TPU v7x, 32 devices: a whole 2x2x4 slice. The times are simulated.
32 devices in a mesh: dp: 8 (over z, y), mp: 4 (over x, core).
Axes of the slice: x: 2, y: 2, z: 4, core: 2. Of those that a mesh axis runs over, the one named last changes fastest.
Arguments:
- tokens: bfloat16 [32768, 512], P(('dp', 'mp')), may hold values from -6 to 6
- cotangent: bfloat16 [32768, 512], P(('dp', 'mp')), may hold values from -6 to 6
- clip_ids: int32 [32768], P('dp'), may hold values from 15 to 511, as said below
- frame_ids: int32 [32768], P('dp'), may hold values from 0 to 15, as said below
- step: int32 [1], replicated, may hold values from 2 to 20
- w_qkv: float32 [3, 512, 512], P(None, 'dp', 'mp'), may hold values from -0.25 to 0.25
- w_out: float32 [512, 512], P('mp', 'dp'), may hold values from -0.75 to 0.75
- w_up: float32 [512, 2048], P('dp', 'mp'), may hold values from -0.25 to 0.25
- w_down: float32 [2048, 512], P('mp', 'dp'), may hold values from -0.125 to 0.125
- norm_params: float32 [4, 512], replicated, may hold values from -0.9 to 1.45, as said below
- moment_qkv: float32 [3, 512, 512], P(None, 'dp', 'mp'), may hold values from -0.00036621094 to 0.00036621094
- moment_out: float32 [512, 512], P('mp', 'dp'), may hold values from -0.00036621094 to 0.00036621094
- moment_up: float32 [512, 2048], P('dp', 'mp'), may hold values from -0.00036621094 to 0.00036621094
- moment_down: float32 [2048, 512], P('mp', 'dp'), may hold values from -0.00036621094 to 0.00036621094
- moment_norm: float32 [4, 512], replicated, may hold values from -0.0009765625 to 0.0009765625
- square_qkv: float32 [3, 512, 512], P(None, 'dp', 'mp'), may hold values from 1.588423e-08 to 6.353692e-08
- square_out: float32 [512, 512], P('mp', 'dp'), may hold values from 1.588423e-08 to 6.353692e-08
- square_up: float32 [512, 2048], P('dp', 'mp'), may hold values from 1.588423e-08 to 6.353692e-08
- square_down: float32 [2048, 512], P('mp', 'dp'), may hold values from 1.588423e-08 to 6.353692e-08
- square_norm: float32 [4, 512], replicated, may hold values from 1.4295807e-07 to 5.718323e-07
- average_qkv: float32 [3, 512, 512], P(None, 'dp', 'mp'), may hold values from -0.25 to 0.25
- average_out: float32 [512, 512], P('mp', 'dp'), may hold values from -0.75 to 0.75
- average_up: float32 [512, 2048], P('dp', 'mp'), may hold values from -0.25 to 0.25
- average_down: float32 [2048, 512], P('mp', 'dp'), may hold values from -0.125 to 0.125
- average_norm: float32 [4, 512], replicated, may hold values from 0.5 to 1.5
Outputs:
- block_out: bfloat16 [32768, 512], P(('dp', 'mp'))
- grad_tokens: float32 [32768, 512], P(('dp', 'mp'))
- grad_norm: float32 [], replicated
- new_qkv: float32 [3, 512, 512], P(None, 'dp', 'mp')
- new_out: float32 [512, 512], P('mp', 'dp')
- new_up: float32 [512, 2048], P('dp', 'mp')
- new_down: float32 [2048, 512], P('mp', 'dp')
- new_norm: float32 [4, 512], replicated
- new_moment_qkv: float32 [3, 512, 512], P(None, 'dp', 'mp')
- new_moment_out: float32 [512, 512], P('mp', 'dp')
- new_moment_up: float32 [512, 2048], P('dp', 'mp')
- new_moment_down: float32 [2048, 512], P('mp', 'dp')
- new_moment_norm: float32 [4, 512], replicated
- new_square_qkv: float32 [3, 512, 512], P(None, 'dp', 'mp')
- new_square_out: float32 [512, 512], P('mp', 'dp')
- new_square_up: float32 [512, 2048], P('dp', 'mp')
- new_square_down: float32 [2048, 512], P('mp', 'dp')
- new_square_norm: float32 [4, 512], replicated
- copy_qkv: bfloat16 [3, 512, 512], P(None, 'dp', 'mp')
- copy_out: bfloat16 [512, 512], P('mp', 'dp')
- copy_up: bfloat16 [512, 2048], P('dp', 'mp')
- copy_down: bfloat16 [2048, 512], P('mp', 'dp')
- new_average_qkv: float32 [3, 512, 512], P(None, 'dp', 'mp')
- new_average_out: float32 [512, 512], P('mp', 'dp')
- new_average_up: float32 [512, 2048], P('dp', 'mp')
- new_average_down: float32 [2048, 512], P('mp', 'dp')
- new_average_norm: float32 [4, 512], replicated
Inputs may be any that keep to these rules, and one draw needn't show every extreme that they name: `clip_ids`: clips are runs of whole frames of 64 tokens with at most 1024 tokens; no clip crosses a boundary between aligned groups of 4096 tokens, and in every such group some clip has exactly 1024 tokens. A clip's number is the index, among all frames of 64 tokens, of its last frame, so numbers never fall along the tokens. `frame_ids`: A token's frame counts whole frames of 64 tokens from the start of its clip. `norm_params`: rows 0 and 2 are gains near one, rows 1 and 3 biases near zero.
All inputs are finite; a program needn't handle non-finite values.
Results may differ from a plain program's by a relative error of at most 0.02.
Values may be sent and summed in bfloat16 or wider, within the bound.
No kernel may reach another device: no remote copies, remote signals or barrier semaphores. Data moves between devices by JAX's collectives and lax.ppermute only.
A program may use at most 128 MiB of HBM per device.

v0:
```python
import jax
import jax.numpy as jnp
from jax import lax
from jax.sharding import PartitionSpec as P

HEAD = 64
CLIP = 1024


norm_eps = 1e-05
beta_one = 0.9
beta_two = 0.95
adam_eps = 1e-08
clip_limit = 1.0
ema_decay = 0.75


def layer_norm(values, gain_row, shift_term):
    center = values - jnp.mean(values, axis=-1, keepdims=True)
    spread = jnp.mean(center * center, axis=-1, keepdims=True)
    return center * lax.rsqrt(spread + norm_eps) * gain_row + shift_term


def adam_update(
    weight, gradient, moment, square, average, step_rate, decay_rate, factor, step_count
):
    gradient = gradient * factor
    moment = beta_one * moment + (1.0 - beta_one) * gradient
    square = beta_two * square + (1.0 - beta_two) * gradient * gradient
    fixed_one = 1.0 - jnp.power(beta_one, step_count)
    fixed_two = 1.0 - jnp.power(beta_two, step_count)
    weight = weight - step_rate * (
        moment / fixed_one / (jnp.sqrt(square / fixed_two) + adam_eps) + decay_rate * weight
    )
    average = ema_decay * average + (1.0 - ema_decay) * weight
    return (weight, moment, square, average)


def per_device(
    tokens,
    cotangent,
    clip_ids,
    frame_ids,
    step,
    w_qkv,
    w_out,
    w_up,
    w_down,
    norm_params,
    moment_qkv,
    moment_out,
    moment_up,
    moment_down,
    moment_norm,
    square_qkv,
    square_out,
    square_up,
    square_down,
    square_norm,
    average_qkv,
    average_out,
    average_up,
    average_down,
    average_norm,
):
    group_rows = clip_ids.shape[0]
    head_width = w_qkv.shape[2]
    heads_here = head_width // HEAD
    full_qkv, full_out, full_up, full_down = (
        lax.all_gather(w_qkv.astype(jnp.bfloat16), "dp", axis=1, tiled=True),
        lax.all_gather(w_out.astype(jnp.bfloat16), "dp", axis=1, tiled=True),
        lax.all_gather(w_up.astype(jnp.bfloat16), "dp", axis=0, tiled=True),
        lax.all_gather(w_down.astype(jnp.bfloat16), "dp", axis=1, tiled=True),
    )
    rows_in = tokens.astype(jnp.float32)
    normed_one = layer_norm(rows_in, norm_params[0], norm_params[1]).astype(jnp.bfloat16)
    normed_one_all = lax.all_gather(normed_one, "mp", axis=0, tiled=True)
    project = jnp.einsum(
        "td,sdc->stc", normed_one_all, full_qkv, preferred_element_type=jnp.float32
    ).astype(jnp.bfloat16)
    queries = project[0]
    pad_keys = jnp.concatenate([jnp.zeros((CLIP, head_width), jnp.bfloat16), project[1]])
    pad_values = jnp.concatenate([jnp.zeros((CLIP, head_width), jnp.bfloat16), project[2]])
    pad_clips = jnp.concatenate([jnp.full((CLIP,), -1, jnp.int32), clip_ids])
    pad_frames = jnp.concatenate([jnp.zeros((CLIP,), jnp.int32), frame_ids])
    block_rows = min(1024, group_rows)
    window_rows = block_rows + CLIP
    block_count = group_rows // block_rows
    starts = jnp.arange(block_count, dtype=jnp.int32) * block_rows
    score_scale = HEAD ** (-0.5)

    def window(offset):
        query_block = lax.dynamic_slice_in_dim(queries, offset, block_rows, 0).reshape(
            block_rows, heads_here, HEAD
        )
        key_block = lax.dynamic_slice_in_dim(pad_keys, offset, window_rows, 0).reshape(
            window_rows, heads_here, HEAD
        )
        value_block = lax.dynamic_slice_in_dim(pad_values, offset, window_rows, 0).reshape(
            window_rows, heads_here, HEAD
        )
        clip_query = lax.dynamic_slice_in_dim(clip_ids, offset, block_rows, 0)
        frame_query = lax.dynamic_slice_in_dim(frame_ids, offset, block_rows, 0)
        clip_keys = lax.dynamic_slice_in_dim(pad_clips, offset, window_rows, 0)
        frame_keys = lax.dynamic_slice_in_dim(pad_frames, offset, window_rows, 0)
        visible = (clip_query[:, None] == clip_keys[None, :]) & (
            frame_keys[None, :] <= frame_query[:, None]
        )
        scores = (
            jnp.einsum("qhe,khe->hqk", query_block, key_block, preferred_element_type=jnp.float32)
            * score_scale
        )
        scores = jnp.where(visible[None], scores, -1e30)
        return (query_block, key_block, value_block, visible, scores)

    def forward_block(offset):
        query_block, key_block, value_block, visible, scores = window(offset)
        row_max = jnp.max(scores, axis=-1, keepdims=True)
        weights = jnp.exp(scores - row_max)
        row_total = jnp.sum(weights, axis=-1, keepdims=True)
        probs_low = (weights / row_total).astype(jnp.bfloat16)
        outcome = jnp.einsum(
            "hqk,khe->qhe", probs_low, value_block, preferred_element_type=jnp.float32
        )
        return (
            outcome.astype(jnp.bfloat16).reshape(block_rows, head_width),
            (row_max + jnp.log(row_total))[..., 0],
        )

    mixture, log_total = lax.map(forward_block, starts)
    mixture = mixture.reshape(group_rows, head_width)
    piece = mixture
    attended = lax.psum_scatter(
        jnp.dot(piece, full_out, preferred_element_type=jnp.float32).astype(jnp.bfloat16),
        "mp",
        scatter_dimension=0,
        tiled=True,
    ).astype(jnp.float32)
    middle = rows_in + attended
    normed_two = layer_norm(middle, norm_params[2], norm_params[3]).astype(jnp.bfloat16)
    normed_two_all = lax.all_gather(normed_two, "mp", axis=0, tiled=True)
    hidden = jnp.dot(normed_two_all, full_up, preferred_element_type=jnp.float32)
    active = jax.nn.gelu(hidden).astype(jnp.bfloat16)
    piece = active
    branch_out = lax.psum_scatter(
        jnp.dot(piece, full_down, preferred_element_type=jnp.float32).astype(jnp.bfloat16),
        "mp",
        scatter_dimension=0,
        tiled=True,
    ).astype(jnp.float32)
    block_out = (middle + branch_out).astype(jnp.bfloat16)
    back_all = lax.all_gather(cotangent, "mp", axis=0, tiled=True)
    grad_down = jnp.einsum("tf,td->fd", active, back_all, preferred_element_type=jnp.float32)
    grad_active = jnp.einsum("td,fd->tf", back_all, full_down, preferred_element_type=jnp.float32)
    gelu_back = jax.vjp(jax.nn.gelu, hidden)[1]
    grad_hidden = gelu_back(grad_active)[0].astype(jnp.bfloat16)
    grad_up = jnp.einsum(
        "td,tf->df", normed_two_all, grad_hidden, preferred_element_type=jnp.float32
    )
    piece = grad_hidden
    grad_second = lax.psum_scatter(
        jnp.einsum("tf,df->td", piece, full_up, preferred_element_type=jnp.float32).astype(
            jnp.bfloat16
        ),
        "mp",
        scatter_dimension=0,
        tiled=True,
    ).astype(jnp.float32)
    norm_back_two = jax.vjp(layer_norm, middle, norm_params[2], norm_params[3])[1]
    grad_middle, gain_two_grad, shift_two_grad = norm_back_two(grad_second)
    grad_middle = grad_middle + cotangent.astype(jnp.float32)
    middle_all = lax.all_gather(grad_middle.astype(jnp.bfloat16), "mp", axis=0, tiled=True)
    grad_wout = jnp.einsum("tc,td->cd", mixture, middle_all, preferred_element_type=jnp.float32)
    grad_mixture = jnp.einsum(
        "td,cd->tc", middle_all, full_out, preferred_element_type=jnp.float32
    ).astype(jnp.bfloat16)

    def backward_block(carried, scan_items):
        pad_key_grad, pad_value_grad = carried
        offset, block_log = scan_items
        query_block, key_block, value_block, visible, scores = window(offset)
        probs = jnp.where(visible[None], jnp.exp(scores - block_log[..., None]), 0.0)
        probs_low = probs.astype(jnp.bfloat16)
        grad_block = lax.dynamic_slice_in_dim(grad_mixture, offset, block_rows, 0).reshape(
            block_rows, heads_here, HEAD
        )
        grad_probs = jnp.einsum(
            "qhe,khe->hqk", grad_block, value_block, preferred_element_type=jnp.float32
        )
        inner = jnp.sum(probs * grad_probs, axis=-1, keepdims=True)
        grad_scores = (probs * (grad_probs - inner)).astype(jnp.bfloat16)
        query_grad = (
            jnp.einsum("hqk,khe->qhe", grad_scores, key_block, preferred_element_type=jnp.float32)
            * score_scale
        )
        key_grad = (
            jnp.einsum("hqk,qhe->khe", grad_scores, query_block, preferred_element_type=jnp.float32)
            * score_scale
        )
        value_grad = jnp.einsum(
            "hqk,qhe->khe", probs_low, grad_block, preferred_element_type=jnp.float32
        )
        old_keys = lax.dynamic_slice_in_dim(pad_key_grad, offset, window_rows, 0)
        old_values = lax.dynamic_slice_in_dim(pad_value_grad, offset, window_rows, 0)
        pad_key_grad = lax.dynamic_update_slice_in_dim(
            pad_key_grad, old_keys + key_grad.reshape(window_rows, head_width), offset, 0
        )
        pad_value_grad = lax.dynamic_update_slice_in_dim(
            pad_value_grad, old_values + value_grad.reshape(window_rows, head_width), offset, 0
        )
        return (
            (pad_key_grad, pad_value_grad),
            query_grad.reshape(block_rows, head_width).astype(jnp.bfloat16),
        )

    empty_grads = jnp.zeros((group_rows + CLIP, head_width), jnp.float32)
    (pad_key_grad, pad_value_grad), query_grads = lax.scan(
        backward_block, (empty_grads, empty_grads), (starts, log_total)
    )
    grad_project = jnp.stack(
        [
            query_grads.reshape(group_rows, head_width),
            pad_key_grad[CLIP:].astype(jnp.bfloat16),
            pad_value_grad[CLIP:].astype(jnp.bfloat16),
        ]
    )
    grad_qkv = jnp.einsum(
        "td,stc->sdc", normed_one_all, grad_project, preferred_element_type=jnp.float32
    )
    piece = grad_project
    grad_first = lax.psum_scatter(
        jnp.einsum("stc,sdc->td", piece, full_qkv, preferred_element_type=jnp.float32).astype(
            jnp.bfloat16
        ),
        "mp",
        scatter_dimension=0,
        tiled=True,
    ).astype(jnp.float32)
    norm_back_one = jax.vjp(layer_norm, rows_in, norm_params[0], norm_params[1])[1]
    grad_rows_one, gain_one_grad, shift_one_grad = norm_back_one(grad_first)
    grad_tokens = grad_middle + grad_rows_one
    gain_part = jnp.stack([gain_one_grad, shift_one_grad, gain_two_grad, shift_two_grad])
    grad_qkv, grad_wout, grad_up, grad_down = (
        lax.psum_scatter(
            grad_qkv.astype(jnp.bfloat16), "dp", scatter_dimension=1, tiled=True
        ).astype(jnp.float32),
        lax.psum_scatter(
            grad_wout.astype(jnp.bfloat16), "dp", scatter_dimension=1, tiled=True
        ).astype(jnp.float32),
        lax.psum_scatter(
            grad_up.astype(jnp.bfloat16), "dp", scatter_dimension=0, tiled=True
        ).astype(jnp.float32),
        lax.psum_scatter(
            grad_down.astype(jnp.bfloat16), "dp", scatter_dimension=1, tiled=True
        ).astype(jnp.float32),
    )
    weight_square = (
        jnp.sum(grad_qkv * grad_qkv)
        + jnp.sum(grad_wout * grad_wout)
        + jnp.sum(grad_up * grad_up)
        + jnp.sum(grad_down * grad_down)
    )
    gain_grads = lax.psum(gain_part, ("dp", "mp"))
    gain_square = jnp.sum(gain_grads * gain_grads)
    leader = (lax.axis_index("dp") == 0) & (lax.axis_index("mp") == 0)
    square_sum = lax.psum(weight_square + jnp.where(leader, gain_square, 0.0), ("dp", "mp"))
    norm_value = jnp.sqrt(square_sum)
    factor = jnp.minimum(1.0, clip_limit / (norm_value + 1e-06))
    step_count = step[0].astype(jnp.float32)
    one = adam_update(
        w_qkv, grad_qkv, moment_qkv, square_qkv, average_qkv, 0.03, 0.1, factor, step_count
    )
    two = adam_update(
        w_out, grad_wout, moment_out, square_out, average_out, 0.09, 0.1, factor, step_count
    )
    three = adam_update(
        w_up, grad_up, moment_up, square_up, average_up, 0.03, 0.1, factor, step_count
    )
    four = adam_update(
        w_down, grad_down, moment_down, square_down, average_down, 0.015, 0.1, factor, step_count
    )
    five = adam_update(
        norm_params,
        gain_grads,
        moment_norm,
        square_norm,
        average_norm,
        0.2,
        0.0,
        factor,
        step_count,
    )
    return (
        block_out,
        grad_tokens,
        norm_value,
        one[0],
        two[0],
        three[0],
        four[0],
        five[0],
        one[1],
        two[1],
        three[1],
        four[1],
        five[1],
        one[2],
        two[2],
        three[2],
        four[2],
        five[2],
        one[0].astype(jnp.bfloat16),
        two[0].astype(jnp.bfloat16),
        three[0].astype(jnp.bfloat16),
        four[0].astype(jnp.bfloat16),
        one[3],
        two[3],
        three[3],
        four[3],
        five[3],
    )


def solution(mesh):
    placed = (
        P(("dp", "mp"), None),
        P(("dp", "mp"), None),
        P("dp"),
        P("dp"),
        P(),
        P(None, "dp", "mp"),
        P("mp", "dp"),
        P("dp", "mp"),
        P("mp", "dp"),
        P(),
        P(None, "dp", "mp"),
        P("mp", "dp"),
        P("dp", "mp"),
        P("mp", "dp"),
        P(),
        P(None, "dp", "mp"),
        P("mp", "dp"),
        P("dp", "mp"),
        P("mp", "dp"),
        P(),
        P(None, "dp", "mp"),
        P("mp", "dp"),
        P("dp", "mp"),
        P("mp", "dp"),
        P(),
    )
    return jax.shard_map(
        per_device,
        mesh=mesh,
        in_specs=placed,
        out_specs=(
            P(("dp", "mp"), None),
            P(("dp", "mp"), None),
            P(),
            P(None, "dp", "mp"),
            P("mp", "dp"),
            P("dp", "mp"),
            P("mp", "dp"),
            P(),
            P(None, "dp", "mp"),
            P("mp", "dp"),
            P("dp", "mp"),
            P("mp", "dp"),
            P(),
            P(None, "dp", "mp"),
            P("mp", "dp"),
            P("dp", "mp"),
            P("mp", "dp"),
            P(),
            P(None, "dp", "mp"),
            P("mp", "dp"),
            P("dp", "mp"),
            P("mp", "dp"),
            P(None, "dp", "mp"),
            P("mp", "dp"),
            P("dp", "mp"),
            P("mp", "dp"),
            P(),
        ),
        check_vma=False,
    )
```

profile of v0, /device:TPU:0, one launch (start us, length us, event | category | flops | bytes accessed | tf_op | source)
XLA Modules:
  0.0 1079.5 jit_solution(7450057246158959648)
XLA Ops:
  15.3 34.3 %all_gather.26 = bf16[128,512]{0,1:T(8,128)(2,1)} all-gather(bf16[128,64]{0,1:T(8,128)(2,1)S(1)} %convert_element_type.150), channel_id=1, replica_groups=mesh['dp'=8,'mp'=4] {'dp'}, dimensions={1}, use_global_device_ids=true | all-gather | bytes 147456 | tf_op jit(solution)/shard_map/all_gather | solution.py:71
  49.6 31.0 %all_gather.25 = bf16[3,512,128]{2,1,0:T(8,128)(2,1)S(1)} all-gather(bf16[3,64,128]{2,1,0:T(8,128)(2,1)S(1)} %convert_element_type.147), channel_id=1, replica_groups=mesh['dp'=8,'mp'=4] {'dp'}, dimensions={1}, use_global_device_ids=true | all-gather | bytes 442368 | tf_op jit(solution)/shard_map/all_gather | solution.py:70
  91.9 93.9 %while.26 = (s32[]{:T(128)}, bf16[4,1024,128]{2,1,0:T(8,128)(2,1)S(1)}, f32[4,2,1024]{2,1,0:T(2,128)}, s32[4]{0:T(128)S(1)}, bf16[5120,128]{0,1:T(8,128)(2,1)}, ...) while((s32[]{:T(128)}, ...), condition=%wide.region_5.6_spmd, body=%wide.region_2.5_spmd.sunk | while | flops 1130493952 | bytes 64102652 | solution.py:130
  191.3 44.3 %reduce-scatter.8.cloned.1.call-done = bf16[1024,512]{1,0:T(8,128)(2,1)} async-done(((bf16[4096,512]{1,0:T(8,128)(2,1)}), bf16[1024,512]{1,0:T(8,128)(2,1)}) %reduce-scatter.8.cloned.1.call-update) | async-done | bytes 1048592 | tf_op jit(solution)/shard_map/reduce_scatter | solution.py:133
  242.5 33.7 %all_gather.29 = bf16[512,512]{0,1:T(8,128)(2,1)} all-gather(bf16[512,64]{0,1:T(8,128)(2,1)S(1)} %convert_element_type.156), channel_id=1, replica_groups=mesh['dp'=8,'mp'=4] {'dp'}, dimensions={1}, use_global_device_ids=true | all-gather | bytes 589824 | tf_op jit(solution)/shard_map/all_gather | solution.py:73
  276.3 33.4 %all_gather.28 = bf16[512,512]{1,0:T(8,128)(2,1)} all-gather(bf16[64,512]{1,0:T(8,128)(2,1)S(1)} %convert_element_type.154), channel_id=1, replica_groups=mesh['dp'=8,'mp'=4] {'dp'}, dimensions={0}, use_global_device_ids=true | all-gather | bytes 589824 | tf_op jit(solution)/shard_map/all_gather | solution.py:72
  317.6 12.1 %fusion.15 = (bf16[4096,512]{1,0:T(8,128)(2,1)S(1)}, f32[4096,512]{1,0:T(8,128)}) fusion(f32[4096,512]{1,0:T(8,128)} %fusion.80, bf16[4096,512]{1,0:T(8,128)(2,1)} %all-gather.7.cloned.1.call-done, bf16[512,512]{1,0:T(8,128)(2,1)} %all_gather.28), kind=kOutput, calls=%fused_computation.42 | convolution fusion | flops 2189426688 | bytes 25690112 | tf_op jit(solution)/shard_map/dot_general | solution.py:142
  345.3 35.7 %reduce-scatter.12.cloned.1.call-done = bf16[1024,512]{1,0:T(8,128)(2,1)} async-done(((bf16[4096,512]{1,0:T(8,128)(2,1)}), bf16[1024,512]{1,0:T(8,128)(2,1)}) %reduce-scatter.12.cloned.1.call-update) | async-done | bytes 1048592 | tf_op jit(solution)/shard_map/reduce_scatter | solution.py:161
  384.0 44.0 %reduce-scatter.10.cloned.1.call-done = bf16[1024,512]{1,0:T(8,128)(2,1)} async-done(((bf16[4096,512]{1,0:T(8,128)(2,1)}), bf16[1024,512]{1,0:T(8,128)(2,1)}) %reduce-scatter.10.cloned.1.call-update) | async-done | bytes 1048592 | tf_op jit(solution)/shard_map/reduce_scatter | solution.py:145
  450.7 18.0 %all-gather.11.cloned.1.call-done = bf16[4096,512]{1,0:T(8,128)(2,1)} async-done(((bf16[1024,512]{1,0:T(8,128)(2,1)}), bf16[4096,512]{1,0:T(8,128)(2,1)}) %all-gather.11.cloned.1.call-update) | async-done | bytes 4194320 | tf_op jit(solution)/shard_map/all_gather | solution.py:172
  477.6 301.9 %while.27 = (s32[]{:T(128)}, f32[5120,128]{1,0:T(8,128)}, f32[5120,128]{1,0:T(8,128)}, bf16[4,1024,128]{2,1,0:T(8,128)(2,1)}, s32[4]{0:T(128)S(1)}, /*index=5*/b...) while((s32[]{:T(128)}, f32[5120,128]{1,0:T(8,128)}, ...), condition=%wide.region_15.16_spmd, body=%wide.region_13.15_spmd.sunk | while | flops 2733635584 | bytes 250987008 | solution.py:217
  505.0 13.4 %multiply_reduce_fusion.4 = (f32[2,1024]{1,0:T(2,128)S(1)}, f32[2,1024,2048]{2,1,0:T(8,128)}) fusion(f32[2,1024,2048]{2,1,0:T(8,128)} %fusion.146, f32[2,1024]{1,0:T(2,128)S(1)} %dynamic-slice_bitcast_fusion.2, bf16[1024,2,64]{0,2,1:T(8,128)(2,1)S(1)} %bitcast.149, bf16[2048,2,64]{0,2,1:T(8,128)(2,1)S(1)} %bitcast.154, ...), kind=kOutput, calls=%fused_computation.16.clone.1 | convolution fusion | flops 562034688 | bytes 36454400 | tf_op jit(solution)/shard_map/while/body/eval_jaxpr/qhe,khe->hqk/dot_general | solution.py:110
  518.4 11.6 %multiply_convert_fusion.5 = bf16[2,1024,2048]{2,1,0:T(8,128)(2,1)S(1)} fusion(f32[2,1024,2048]{2,1,0:T(8,128)} %get-tuple-element.614, f32[2,1024,2048]{2,1,0:T(8,128)} %fusion.146, f32[2,1024]{1,0:T(2,128)S(1)} %get-tuple-element.615), kind=kLoop, calls=%fused_computation.15.clone.1 | loop fusion | flops 12582912 | bytes 41951232 | tf_op jit(solution)/shard_map/while/body/eval_jaxpr/convert_element_type | solution.py:191
  580.7 13.4 %multiply_reduce_fusion.4 = (f32[2,1024]{1,0:T(2,128)S(1)}, f32[2,1024,2048]{2,1,0:T(8,128)}) fusion(f32[2,1024,2048]{2,1,0:T(8,128)} %fusion.146, f32[2,1024]{1,0:T(2,128)S(1)} %dynamic-slice_bitcast_fusion.2, bf16[1024,2,64]{0,2,1:T(8,128)(2,1)S(1)} %bitcast.149, bf16[2048,2,64]{0,2,1:T(8,128)(2,1)S(1)} %bitcast.154, ...), kind=kOutput, calls=%fused_computation.16.clone.1 | convolution fusion | flops 562034688 | bytes 36454400 | tf_op jit(solution)/shard_map/while/body/eval_jaxpr/qhe,khe->hqk/dot_general | solution.py:110
  594.2 11.5 %multiply_convert_fusion.5 = bf16[2,1024,2048]{2,1,0:T(8,128)(2,1)S(1)} fusion(f32[2,1024,2048]{2,1,0:T(8,128)} %get-tuple-element.614, f32[2,1024,2048]{2,1,0:T(8,128)} %fusion.146, f32[2,1024]{1,0:T(2,128)S(1)} %get-tuple-element.615), kind=kLoop, calls=%fused_computation.15.clone.1 | loop fusion | flops 12582912 | bytes 41951232 | tf_op jit(solution)/shard_map/while/body/eval_jaxpr/convert_element_type | solution.py:191
  656.4 13.4 %multiply_reduce_fusion.4 = (f32[2,1024]{1,0:T(2,128)S(1)}, f32[2,1024,2048]{2,1,0:T(8,128)}) fusion(f32[2,1024,2048]{2,1,0:T(8,128)} %fusion.146, f32[2,1024]{1,0:T(2,128)S(1)} %dynamic-slice_bitcast_fusion.2, bf16[1024,2,64]{0,2,1:T(8,128)(2,1)S(1)} %bitcast.149, bf16[2048,2,64]{0,2,1:T(8,128)(2,1)S(1)} %bitcast.154, ...), kind=kOutput, calls=%fused_computation.16.clone.1 | convolution fusion | flops 562034688 | bytes 36454400 | tf_op jit(solution)/shard_map/while/body/eval_jaxpr/qhe,khe->hqk/dot_general | solution.py:110
  669.8 11.5 %multiply_convert_fusion.5 = bf16[2,1024,2048]{2,1,0:T(8,128)(2,1)S(1)} fusion(f32[2,1024,2048]{2,1,0:T(8,128)} %get-tuple-element.614, f32[2,1024,2048]{2,1,0:T(8,128)} %fusion.146, f32[2,1024]{1,0:T(2,128)S(1)} %get-tuple-element.615), kind=kLoop, calls=%fused_computation.15.clone.1 | loop fusion | flops 12582912 | bytes 41951232 | tf_op jit(solution)/shard_map/while/body/eval_jaxpr/convert_element_type | solution.py:191
  731.9 13.4 %multiply_reduce_fusion.4 = (f32[2,1024]{1,0:T(2,128)S(1)}, f32[2,1024,2048]{2,1,0:T(8,128)}) fusion(f32[2,1024,2048]{2,1,0:T(8,128)} %fusion.146, f32[2,1024]{1,0:T(2,128)S(1)} %dynamic-slice_bitcast_fusion.2, bf16[1024,2,64]{0,2,1:T(8,128)(2,1)S(1)} %bitcast.149, bf16[2048,2,64]{0,2,1:T(8,128)(2,1)S(1)} %bitcast.154, ...), kind=kOutput, calls=%fused_computation.16.clone.1 | convolution fusion | flops 562034688 | bytes 36454400 | tf_op jit(solution)/shard_map/while/body/eval_jaxpr/qhe,khe->hqk/dot_general | solution.py:110
  745.4 11.5 %multiply_convert_fusion.5 = bf16[2,1024,2048]{2,1,0:T(8,128)(2,1)S(1)} fusion(f32[2,1024,2048]{2,1,0:T(8,128)} %get-tuple-element.614, f32[2,1024,2048]{2,1,0:T(8,128)} %fusion.146, f32[2,1024]{1,0:T(2,128)S(1)} %get-tuple-element.615), kind=kLoop, calls=%fused_computation.15.clone.1 | loop fusion | flops 12582912 | bytes 41951232 | tf_op jit(solution)/shard_map/while/body/eval_jaxpr/convert_element_type | solution.py:191
  801.6 44.0 %reduce-scatter.16.cloned.1.call-done = bf16[128,64]{0,1:T(8,128)(2,1)} async-done(((bf16[128,512]{0,1:T(8,128)(2,1)}), bf16[128,64]{0,1:T(8,128)(2,1)}) %reduce-scatter.16.cloned.1.call-update) | async-done | bytes 16400 | tf_op jit(solution)/shard_map/reduce_scatter | solution.py:247
  846.9 73.9 %all-reduce.7.cloned.1.call-done = bf16[3,512,128]{2,0,1:T(4,128)(2,1)} async-done(((bf16[3,512,128]{2,0,1:T(4,128)(2,1)}), bf16[3,512,128]{2,0,1:T(4,128)(2,1)}) %all-reduce.7.cloned.1.call-update) | async-done | bytes 393232
  925.1 42.0 %reduce-scatter.14.cloned.1.call-done = bf16[1024,512]{1,0:T(8,128)(2,1)} async-done(((bf16[4096,512]{1,0:T(8,128)(2,1)}), bf16[1024,512]{1,0:T(8,128)(2,1)}) %reduce-scatter.14.cloned.1.call-update) | async-done | bytes 1048592 | tf_op jit(solution)/shard_map/reduce_scatter | solution.py:231
  973.9 39.6 %psum.14 = f32[4,512]{1,0:T(4,128)S(1)} all-reduce(f32[4,512]{1,0:T(4,128)} %pad_maximum_fusion.7), channel_id=1, replica_groups=mesh['dp'=8,'mp'=4] {'dp','mp'}, use_global_device_ids=true, to_apply=%region_31.32 | all-reduce | flops 2048 | bytes 16384 | tf_op jit(solution)/shard_map/psum | solution.py:263
  1014.7 41.0 %psum.15 = f32[]{:T(128)} all-reduce(f32[]{:T(128)S(6)} %add.267), channel_id=1, replica_groups=mesh['dp'=8,'mp'=4] {'dp','mp'}, use_global_device_ids=true, to_apply=%region_33.34 | all-reduce | flops 1 | bytes 8 | tf_op jit(solution)/shard_map/psum | solution.py:266
  (412 shorter events, 403.9 us)
Async XLA Ops:
  7.2 73.4 %all-gather.5.cloned.1.call-start = ((), (), s32[]{:S(2)}) async-start(), calls=%async_computation.7 | async-start | bytes 5242880 | tf_op jit(solution)/shard_map/all_gather | solution.py:77
  15.2 220.4 %reduce-scatter.8.cloned.1.call-start = ((), (), s32[]{:S(2)}) async-start(), calls=%async_computation.8 | async-start | bytes 5242880 | tf_op jit(solution)/shard_map/reduce_scatter | solution.py:133
  91.9 94.9 %copy-start.16 = (bf16[128,512]{0,1:T(8,128)(2,1)S(1)}, bf16[128,512]{0,1:T(8,128)(2,1)}, u32[]{:S(2)}) copy-start(bf16[128,512]{0,1:T(8,128)(2,1)} %all_gather.26) | copy-start | bytes 393220
  189.9 45.6 %copy-start.1 = (bf16[1024,512]{1,0:T(8,128)(2,1)S(1)}, bf16[1024,512]{1,0:T(8,128)(2,1)}, u32[]{:S(2)}) copy-start(bf16[1024,512]{1,0:T(8,128)(2,1)} %param.29) | copy-start | bytes 3145732
  190.0 119.7 %all-gather.9.cloned.1.call-start = ((), (), s32[]{:S(2)}) async-start(), calls=%async_computation.11 | async-start | bytes 5242880 | tf_op jit(solution)/shard_map/all_gather | solution.py:152
  190.7 51.8 %copy-start.18 = (f32[64,512]{1,0:T(8,128)S(1)}, f32[64,512]{1,0:T(8,128)}, u32[]{:S(2)}) copy-start(f32[64,512]{1,0:T(8,128)} %param.36) | copy-start | bytes 393220
  190.7 51.8 %copy-start.20 = (f32[512,64]{0,1:T(8,128)S(1)}, f32[512,64]{0,1:T(8,128)}, u32[]{:S(2)}) copy-start(f32[512,64]{0,1:T(8,128)} %param.37) | copy-start | bytes 393220
  190.7 126.8 %all-gather.7.cloned.1.call-start = ((), (), s32[]{:S(2)}) async-start(), calls=%async_computation.9 | async-start | bytes 5242880 | tf_op jit(solution)/shard_map/all_gather | solution.py:141
  242.4 138.6 %reduce-scatter.12.cloned.1.call-start = ((), (), s32[]{:S(2)}) async-start(), calls=%async_computation.12 | async-start | bytes 5242880 | tf_op jit(solution)/shard_map/reduce_scatter | solution.py:161
  336.1 91.8 %reduce-scatter.10.cloned.1.call-start = ((), (), s32[]{:S(2)}) async-start(), calls=%async_computation.10 | async-start | bytes 5242880 | tf_op jit(solution)/shard_map/reduce_scatter | solution.py:145
  345.3 123.3 %all-gather.11.cloned.1.call-start = ((), (), s32[]{:S(2)}) async-start(), calls=%async_computation.13 | async-start | bytes 5242880 | tf_op jit(solution)/shard_map/all_gather | solution.py:172
  434.0 364.6 %reduce-scatter.18.cloned.1.call-start = ((), (), s32[]{:S(2)}) async-start(), calls=%async_computation.16 | async-start | bytes 589824 | tf_op jit(solution)/shard_map/reduce_scatter | solution.py:250
  440.7 359.4 %reduce-scatter.20.cloned.1.call-start = ((), (), s32[]{:S(2)}) async-start(), calls=%async_computation.17 | async-start | bytes 589824 | tf_op jit(solution)/shard_map/reduce_scatter | solution.py:253
  450.6 395.0 %reduce-scatter.16.cloned.1.call-start = ((), (), s32[]{:S(2)}) async-start(), calls=%async_computation.15 | async-start | bytes 147456 | tf_op jit(solution)/shard_map/reduce_scatter | solution.py:247
  784.5 136.3 %all-reduce.7.cloned.1.call-start = ((), (), s32[]{:S(2)}) async-start(), calls=%async_computation.18 | async-start | bytes 1048576
  791.0 176.1 %reduce-scatter.14.cloned.1.call-start = ((), (), s32[]{:S(2)}) async-start(), calls=%async_computation.14 | async-start | bytes 5242880 | tf_op jit(solution)/shard_map/reduce_scatter | solution.py:231
  796.4 170.7 %copy-start.2 = (bf16[1024,512]{1,0:T(8,128)(2,1)S(1)}, bf16[1024,512]{1,0:T(8,128)(2,1)}, u32[]{:S(2)}) copy-start(bf16[1024,512]{1,0:T(8,128)(2,1)} %param.29) | copy-start | bytes 3145732
  796.4 170.7 %copy-start.34 = (f32[1024]{0:T(1024)S(1)}, f32[1024]{0:T(1024)}, u32[]{:S(2)}) copy-start(f32[1024]{0:T(1024)} %copy-done.33) | copy-start | bytes 12292
  796.4 170.7 %copy-start.44 = (f32[1,512]{1,0:T(1,128)S(1)}, f32[1,512]{1,0:T(1,128)}, u32[]{:S(2)}) copy-start(f32[1,512]{1,0:T(1,128)} %copy-done.43) | copy-start | bytes 6148
  796.4 173.3 %copy-start.40 = (f32[1024]{0:T(1024)S(1)}, f32[1024]{0:T(1024)}, u32[]{:S(2)}) copy-start(f32[1024]{0:T(1024)} %copy-done.39) | copy-start | bytes 12292
  796.4 265.5 %copy-start.19 = (f32[64,512]{1,0:T(8,128)S(1)}, f32[64,512]{1,0:T(8,128)}, u32[]{:S(2)}) copy-start(f32[64,512]{1,0:T(8,128)} %param.36) | copy-start | bytes 393220
  796.4 268.0 %copy-start.21 = (f32[512,64]{0,1:T(8,128)S(1)}, f32[512,64]{0,1:T(8,128)}, u32[]{:S(2)}) copy-start(f32[512,64]{0,1:T(8,128)} %param.37) | copy-start | bytes 393220
  798.5 263.3 %copy-start.30 = (bf16[64,512]{1,0:T(8,128)(2,1)S(1)}, bf16[64,512]{1,0:T(8,128)(2,1)}, u32[]{:S(2)}) copy-start(bf16[64,512]{1,0:T(8,128)(2,1)} %reduce-scatter.18.cloned.1.call-done) | copy-start | bytes 196612
  922.3 146.0 %copy-start.9 = (f32[1024,512]{1,0:T(8,128)S(1)}, f32[1024,512]{1,0:T(8,128)}, u32[]{:S(2)}) copy-start(f32[1024,512]{1,0:T(8,128)} %copy-done.8) | copy-start | bytes 6291460
  (65 other events, 616.5 us)
Sparse Core Ops, SparseCore 0:
  15.3 37.1 all-gather.4
  190.1 45.4 reduce-scatter.7
  237.2 34.4 all-gather.8
  273.8 34.4 all-gather.6
  336.3 44.7 reduce-scatter.11
  383.4 44.4 reduce-scatter.9
  434.1 34.4 all-gather.10
  472.3 61.9 reduce-scatter.17
  537.6 60.8 reduce-scatter.19
  784.6 60.9 reduce-scatter.15
  849.4 71.3 all-reduce.6
  923.2 43.7 reduce-scatter.13
where the time goes:
time: 1090 us; the launch traced here: 1080 us
  waiting for transfers between devices  303 us (28%)
  matrix products  232 us (21%)
  blocking collectives  213 us (20%)
  local copies, waits for them, and re-layouts  141 us (13%)
  other arithmetic  140 us (13%)
  loops' own time  27.2 us (2%)
  between operations  21.7 us (2%)
    unnamed x13, waiting for transfers between devices  74.8 us
    dot_general x8, matrix products, window(): jnp.einsum('qhe,khe->hqk', query_block, key_block, preferred_element_type...  69.3 us
    convert_element_type x4, other arithmetic, backward_block(): grad_scores = (probs * (grad_probs - inner)).astype(jnp.bfloat16)  46 us
    reduce_scatter x1, waiting for transfers between devices, per_device(): lax.psum_scatter(jnp.dot(piece, full_out, preferred_element_type=jnp.floa...  44.3 us
    reduce_scatter x1, waiting for transfers between devices, per_device(): lax.psum_scatter(grad_wout.astype(jnp.bfloat16), 'dp', scatter_dimension=...  44 us
    reduce_scatter x1, waiting for transfers between devices, per_device(): lax.psum_scatter(jnp.dot(piece, full_down, preferred_element_type=jnp.flo...  44 us
    reduce_scatter x1, waiting for transfers between devices, per_device(): lax.psum_scatter(jnp.einsum('stc,sdc->td', piece, full_qkv, preferred_ele...  42 us
    psum x1, blocking collectives, per_device(): lax.psum(weight_square + jnp.where(leader, gain_square, 0.0), ('dp', 'mp'))  41 us
  transfers between devices with their start and end apart: 12, of which 7 were waited for; matrix products, arithmetic and copies ran while one was open for 32% of the time, Pallas kernels for 0%

commit v1 on v0

v1 whole, which is shorter than its diff:
```python
import functools

import jax
import jax.numpy as jnp
from jax import lax
from jax.experimental import pallas as pl
from jax.experimental.pallas import tpu as pltpu
from jax.sharding import PartitionSpec as P

HEAD = 64
CLIP = 1024
FRAME = 64

norm_eps = 1e-05
beta_one = 0.9
beta_two = 0.95
adam_eps = 1e-08
clip_limit = 1.0
ema_decay = 0.75

F32 = jnp.float32
BF16 = jnp.bfloat16
BOTH = ("dp", "mp")
VMEM = pltpu.VMEM
MASKED = -1e30
TQ = 128
TK = 256
ROWS = 256


def mm(a, b):
    return lax.dot_general(a, b, (((1,), (0,)), ((), ())), preferred_element_type=F32)


def mm_nt(a, b):
    return lax.dot_general(a, b, (((1,), (1,)), ((), ())), preferred_element_type=F32)


def mm_tn(a, b):
    return lax.dot_general(a, b, (((0,), (0,)), ((), ())), preferred_element_type=F32)


def call(body, outs, ins, scratch=(), smem=0, flops=0, moved=0):
    return pl.pallas_call(
        body,
        out_shape=outs,
        in_specs=[pl.BlockSpec(memory_space=pltpu.SMEM)] * smem
        + [pl.BlockSpec(memory_space=VMEM)] * (len(ins) - smem),
        out_specs=jax.tree.map(lambda _: pl.BlockSpec(memory_space=VMEM), outs),
        scratch_shapes=list(scratch),
        compiler_params=pltpu.CompilerParams(vmem_limit_bytes=60 << 20),
        cost_estimate=pl.CostEstimate(flops=flops, bytes_accessed=moved, transcendentals=0),
    )(*ins)


def normalize(rows):
    center = rows - jnp.mean(rows, axis=-1, keepdims=True)
    inverse = lax.rsqrt(jnp.mean(center * center, axis=-1, keepdims=True) + norm_eps)
    return center * inverse, inverse


def norm_back(grad, xhat, inverse, gain_row):
    gy = grad * gain_row
    return inverse * (
        gy
        - jnp.mean(gy, axis=-1, keepdims=True)
        - xhat * jnp.mean(gy * xhat, axis=-1, keepdims=True)
    )


def project_body(own_ref, halo_ref, norm_ref, w_ref, q_ref, k_ref, v_ref, kt_ref, vt_ref, xn_ref):
    gain, shift = norm_ref[0:1, :], norm_ref[1:2, :]

    def rows_of(ref, tile, base, with_query):
        at = pl.ds(pl.multiple_of(tile * ROWS, ROWS), ROWS)
        to = pl.ds(pl.multiple_of(base + tile * ROWS, ROWS), ROWS)
        xhat, _ = normalize(ref[at, :].astype(F32))
        xn = (xhat * gain + shift).astype(BF16)
        xn_ref[to, :] = xn
        if with_query:
            q_ref[at, :] = (mm(xn, w_ref[0]).astype(BF16).astype(F32) * HEAD**-0.5).astype(BF16)
        k = mm(xn, w_ref[1])
        v = mm(xn, w_ref[2])
        k_ref[to, :] = k.astype(BF16)
        v_ref[to, :] = v.astype(BF16)
        kt_ref[:, to] = k.T.astype(BF16)
        vt_ref[:, to] = v.T.astype(BF16)

    @pl.loop(0, CLIP // ROWS)
    def _(tile):
        rows_of(halo_ref, tile, 0, False)

    @pl.loop(0, own_ref.shape[0] // ROWS)
    def _(tile):
        rows_of(own_ref, tile, CLIP, True)


def project(own, halo, norms, w_qkv):
    n, d = own.shape
    total = n + CLIP
    shape = jax.ShapeDtypeStruct
    return call(
        project_body,
        (
            shape((n, d), BF16),
            shape((total, d), BF16),
            shape((total, d), BF16),
            shape((d, total), BF16),
            shape((d, total), BF16),
            shape((total, d), BF16),
        ),
        (own, halo, norms, w_qkv),
        flops=2 * d * d * (2 * total + n),
        moved=2 * d * (6 * total + 3 * n),
    )


def split_heads(pair, rows):
    lane = lax.broadcasted_iota(jnp.int32, (rows, 2 * HEAD), 1)
    zero = jnp.zeros_like(pair)
    return jnp.concatenate([jnp.where(lane < HEAD, pair, zero), jnp.where(lane < HEAD, zero, pair)])


def seen(low_row, query_tile, key_tile):
    shape = (TK, 2 * TQ)
    key_frame = (key_tile * TK + lax.broadcasted_iota(jnp.int32, shape, 0)) // FRAME
    spot = lax.rem(lax.broadcasted_iota(jnp.int32, shape, 1), TQ)
    query_frame = (CLIP + query_tile * TQ + spot) // FRAME
    return (key_frame >= low_row) & (key_frame <= query_frame)


def attend_body(first_ref, low_ref, q_ref, k_ref, vt_ref, mix_ref, log_ref, qz, acc, top, total):
    pairs = q_ref.shape[1] // (2 * HEAD)

    @pl.loop(0, q_ref.shape[0] // TQ)
    def _(i):
        at = pl.ds(pl.multiple_of(i * TQ, TQ), TQ)
        low = low_ref[0:1, at]
        low = jnp.concatenate([low, low], axis=1)
        for p in range(pairs):
            qz[p] = split_heads(q_ref[at, p * 128 : (p + 1) * 128], TQ)
        acc[...] = jnp.zeros_like(acc)
        top[...] = jnp.full_like(top, MASKED)
        total[...] = jnp.zeros_like(total)

        def step(j, carry):
            keys = pl.ds(pl.multiple_of(j * TK, TK), TK)
            visible = seen(low, i, j)
            for p in range(pairs):
                lanes = slice(p * 128, (p + 1) * 128)
                scores = jnp.where(visible, mm_nt(k_ref[keys, lanes], qz[p]), MASKED)
                old = top[p]
                new = jnp.maximum(old, jnp.max(scores, axis=0, keepdims=True))
                weights = jnp.exp(scores - new)
                keep = jnp.exp(old - new)
                top[p] = new
                total[p] = total[p] * keep + jnp.sum(weights, axis=0, keepdims=True)
                low_weights = weights.astype(BF16)
                for h in range(2):
                    half = slice(h * HEAD, (h + 1) * HEAD)
                    wide = slice(h * TQ, (h + 1) * TQ)
                    values = vt_ref[p * 128 + h * HEAD : p * 128 + (h + 1) * HEAD, keys]
                    acc[p, half, :] = acc[p, half, :] * keep[:, wide] + mm(
                        values, low_weights[:, wide]
                    )
            return carry

        lax.fori_loop(first_ref[i], pl.cdiv(CLIP + (i + 1) * TQ, TK), step, 0)
        for p in range(pairs):
            sums = total[p]
            for h in range(2):
                half = slice(h * HEAD, (h + 1) * HEAD)
                wide = slice(h * TQ, (h + 1) * TQ)
                acc[p, half, :] = acc[p, half, :] / sums[:, wide]
                log_ref[2 * p + h : 2 * p + h + 1, at] = top[p][:, wide] + jnp.log(sums[:, wide])
            mix_ref[at, p * 128 : (p + 1) * 128] = acc[p].T.astype(BF16)


def attend(first, low, q, k, vt):
    n, d = q.shape
    pairs = d // 128
    return call(
        attend_body,
        (jax.ShapeDtypeStruct((n, d), BF16), jax.ShapeDtypeStruct((d // HEAD, n), F32)),
        (first, low, q, k, vt),
        scratch=(
            VMEM((pairs, 2 * TQ, 128), BF16),
            VMEM((pairs, 128, TQ), F32),
            VMEM((pairs, 1, 2 * TQ), F32),
            VMEM((pairs, 1, 2 * TQ), F32),
        ),
        smem=1,
        flops=8 * n * 1024 * d,
        moved=2 * d * (2 * n + 4 * k.shape[0]),
    )


def attend_back_body(
    first_ref, low_ref, q_ref, k_ref, v_ref, kt_ref, mix_ref, log_ref, grad_ref,
    dq_ref, dk_ref, dv_ref, qz, gz, acc, dk_acc, dv_acc,
):
    pairs = q_ref.shape[1] // (2 * HEAD)
    dk_acc[...] = jnp.zeros_like(dk_acc)
    dv_acc[...] = jnp.zeros_like(dv_acc)

    @pl.loop(0, q_ref.shape[0] // TQ)
    def _(i):
        at = pl.ds(pl.multiple_of(i * TQ, TQ), TQ)
        low = low_ref[0:1, at]
        low = jnp.concatenate([low, low], axis=1)
        logs, inners = [], []
        for p in range(pairs):
            lanes = slice(p * 128, (p + 1) * 128)
            grad = grad_ref[at, lanes]
            qz[p] = split_heads(q_ref[at, lanes], TQ)
            gz[p] = split_heads(grad, TQ)
            both = (grad.astype(F32) * mix_ref[at, lanes].astype(F32)).T
            inners.append(
                jnp.concatenate(
                    [
                        jnp.sum(both[:HEAD], axis=0, keepdims=True),
                        jnp.sum(both[HEAD:], axis=0, keepdims=True),
                    ],
                    axis=1,
                )
            )
            logs.append(
                jnp.concatenate(
                    [log_ref[2 * p : 2 * p + 1, at], log_ref[2 * p + 1 : 2 * p + 2, at]], axis=1
                )
            )
        acc[...] = jnp.zeros_like(acc)

        def step(j, carry):
            keys = pl.ds(pl.multiple_of(j * TK, TK), TK)
            visible = seen(low, i, j)
            for p in range(pairs):
                lanes = slice(p * 128, (p + 1) * 128)
                scores = jnp.where(visible, mm_nt(k_ref[keys, lanes], qz[p]), MASKED)
                probs = jnp.exp(scores - logs[p])
                grad_probs = mm_nt(v_ref[keys, lanes], gz[p])
                grad_scores = (probs * (grad_probs - inners[p])).astype(BF16)
                dv_acc[keys, lanes] += mm(probs.astype(BF16), gz[p])
                dk_acc[keys, lanes] += mm(grad_scores, qz[p])
                for h in range(2):
                    half = slice(h * HEAD, (h + 1) * HEAD)
                    wide = slice(h * TQ, (h + 1) * TQ)
                    rows = kt_ref[p * 128 + h * HEAD : p * 128 + (h + 1) * HEAD, keys]
                    acc[p, half, :] += mm(rows, grad_scores[:, wide])
            return carry

        lax.fori_loop(first_ref[i], pl.cdiv(CLIP + (i + 1) * TQ, TK), step, 0)
        for p in range(pairs):
            dq_ref[at, p * 128 : (p + 1) * 128] = (acc[p].T * HEAD**-0.5).astype(BF16)

    dk_ref[...] = dk_acc[...].astype(BF16)
    dv_ref[...] = dv_acc[...].astype(BF16)


def attend_back(first, low, q, k, v, kt, mixture, logs, grad):
    n, d = q.shape
    total = k.shape[0]
    pairs = d // 128
    shape = jax.ShapeDtypeStruct
    return call(
        attend_back_body,
        (shape((n, d), BF16), shape((total, d), BF16), shape((total, d), BF16)),
        (first, low, q, k, v, kt, mixture, logs, grad),
        scratch=(
            VMEM((pairs, 2 * TQ, 128), BF16),
            VMEM((pairs, 2 * TQ, 128), BF16),
            VMEM((pairs, 128, TQ), F32),
            VMEM((total, d), F32),
            VMEM((total, d), F32),
        ),
        smem=1,
        flops=20 * n * 1024 * d,
        moved=2 * d * (4 * n + 5 * total),
    )


def feed_body(
    x_ref, mix_ref, cot_ref, norm_ref, wo_ref, up_ref, down_ref,
    out_ref, gmix_ref, gmid_ref, low_ref, n2_ref, act_ref, gh_ref, gain_ref,
):
    gain, shift = norm_ref[2:3, :], norm_ref[3:4, :]
    ff = up_ref.shape[1]
    wide = min(512, ff)
    root = 0.7978845608028654
    gain_ref[...] = jnp.zeros_like(gain_ref)

    @pl.loop(0, x_ref.shape[0] // ROWS)
    def _(tile):
        at = pl.ds(pl.multiple_of(tile * ROWS, ROWS), ROWS)
        cot = cot_ref[at, :]
        middle = x_ref[at, :].astype(F32) + mm_nt(mix_ref[at, :], wo_ref[...])
        xhat, inverse = normalize(middle)
        n2 = (xhat * gain + shift).astype(BF16)
        n2_ref[at, :] = n2
        out = middle
        second = jnp.zeros_like(middle)
        for c in range(ff // wide):
            cols = slice(c * wide, (c + 1) * wide)
            hidden = mm(n2, up_ref[:, cols])
            square = hidden * hidden
            bent = jnp.tanh(root * hidden * (1.0 + 0.044715 * square))
            half = 0.5 * (1.0 + bent)
            active = (hidden * half).astype(BF16)
            slope = half + hidden * (0.5 * root) * (1.0 - bent * bent) * (
                1.0 + (3 * 0.044715) * square
            )
            act_ref[at, cols] = active
            out += mm_nt(active, down_ref[:, cols])
            gh = (mm(cot, down_ref[:, cols]) * slope).astype(BF16)
            gh_ref[at, cols] = gh
            second += mm_nt(gh, up_ref[:, cols])
        out_ref[at, :] = out.astype(BF16)
        gain_ref[0:1, :] += jnp.sum(second * xhat, axis=0, keepdims=True)
        gain_ref[1:2, :] += jnp.sum(second, axis=0, keepdims=True)
        gmid = cot.astype(F32) + norm_back(second, xhat, inverse, gain)
        gmid_ref[at, :] = gmid
        low = gmid.astype(BF16)
        low_ref[at, :] = low
        gmix_ref[at, :] = mm(low, wo_ref[...]).astype(BF16)


def feed(x, mixture, cot, norms, wo, up, down):
    n, d = x.shape
    ff = up.shape[1]
    shape = jax.ShapeDtypeStruct
    return call(
        feed_body,
        (
            shape((n, d), BF16),
            shape((n, d), BF16),
            shape((n, d), F32),
            shape((n, d), BF16),
            shape((n, d), BF16),
            shape((n, ff), BF16),
            shape((n, ff), BF16),
            shape((2, d), F32),
        ),
        (x, mixture, cot, norms, wo, up, down),
        flops=2 * n * d * (4 * ff + 2 * d),
        moved=2 * n * (9 * d + 2 * ff) + 4 * d * ff,
    )


def feed_weights_body(n2_ref, gh_ref, cot_ref, act_ref, low_ref, mix_ref, gup_ref, gdown_ref, gout_ref):
    ff = gh_ref.shape[1]
    wide = min(512, ff)
    for c in range(ff // wide):
        cols = slice(c * wide, (c + 1) * wide)
        gup_ref[:, cols] = mm_tn(n2_ref[...], gh_ref[:, cols]).astype(BF16)
        gdown_ref[:, cols] = mm_tn(cot_ref[...], act_ref[:, cols]).astype(BF16)
    gout_ref[...] = mm_tn(low_ref[...], mix_ref[...]).astype(BF16)


def feed_weights(n2, gh, cot, act, low, mixture):
    n, d = n2.shape
    ff = gh.shape[1]
    shape = jax.ShapeDtypeStruct
    return call(
        feed_weights_body,
        (shape((d, ff), BF16), shape((d, ff), BF16), shape((d, d), BF16)),
        (n2, gh, cot, act, low, mixture),
        flops=2 * n * d * (2 * ff + d),
        moved=2 * n * (4 * d + 2 * ff) + 4 * d * ff,
    )


def project_weights_body(xn_ref, dq_ref, dk_ref, dv_ref, g_ref):
    g_ref[0] = mm_tn(xn_ref[CLIP:, :], dq_ref[...]).astype(BF16)
    g_ref[1] = mm_tn(xn_ref[...], dk_ref[...]).astype(BF16)
    g_ref[2] = mm_tn(xn_ref[...], dv_ref[...]).astype(BF16)


def project_weights(xn, dq, dk, dv):
    n, d = dq.shape
    total = xn.shape[0]
    return call(
        project_weights_body,
        jax.ShapeDtypeStruct((3, d, d), BF16),
        (xn, dq, dk, dv),
        flops=2 * d * d * (2 * total + n),
        moved=2 * d * (3 * total + n) + 6 * d * d,
    )


def first_back_body(own_ref, halo_ref, norm_ref, w_ref, dq_ref, dk_ref, dv_ref, gmid_ref,
                    grad_ref, back_ref, gain_ref):
    gain = norm_ref[0:1, :]
    gain_ref[...] = jnp.zeros_like(gain_ref)

    def rows_of(ref, tile, base, own):
        at = pl.ds(pl.multiple_of(tile * ROWS, ROWS), ROWS)
        to = pl.ds(pl.multiple_of(base + tile * ROWS, ROWS), ROWS)
        first = mm_nt(dk_ref[to, :], w_ref[1]) + mm_nt(dv_ref[to, :], w_ref[2])
        if own:
            first += mm_nt(dq_ref[at, :], w_ref[0])
        xhat, inverse = normalize(ref[at, :].astype(F32))
        gain_ref[0:1, :] += jnp.sum(first * xhat, axis=0, keepdims=True)
        gain_ref[1:2, :] += jnp.sum(first, axis=0, keepdims=True)
        grad = norm_back(first, xhat, inverse, gain)
        if own:
            grad_ref[at, :] = gmid_ref[at, :] + grad
        else:
            back_ref[at, :] = grad.astype(BF16)

    @pl.loop(0, CLIP // ROWS)
    def _(tile):
        rows_of(halo_ref, tile, 0, False)

    @pl.loop(0, own_ref.shape[0] // ROWS)
    def _(tile):
        rows_of(own_ref, tile, CLIP, True)


def first_back(own, halo, norms, w_qkv, dq, dk, dv, gmid):
    n, d = own.shape
    total = n + CLIP
    shape = jax.ShapeDtypeStruct
    return call(
        first_back_body,
        (shape((n, d), F32), shape((CLIP, d), BF16), shape((2, d), F32)),
        (own, halo, norms, w_qkv, dq, dk, dv, gmid),
        flops=2 * d * d * (2 * total + n),
        moved=2 * d * (4 * total + 6 * n),
    )


class Grid:
    def __init__(self, dp, mp):
        self.dp, self.mp = dp, mp
        self.fast = (dp, mp) == (8, 4)

    def pairs(self, move):
        found = []
        for i in range(self.dp * self.mp):
            z, y, x, c = i >> 3, (i >> 2) & 1, (i >> 1) & 1, i & 1
            z, y, x, c = move(z, y, x, c)
            found.append((i, (((z * 2 + y) * 2 + x) * 2 + c)))
        return found

    def spot(self):
        dp, mp = lax.axis_index("dp"), lax.axis_index("mp")
        return dp // 2, dp % 2, mp // 2, mp % 2

    def along_z(self, value, k):
        return lax.ppermute(value, BOTH, self.pairs(lambda z, y, x, c: ((z + k) % 4, y, x, c)))

    def second(self, value):
        return lax.ppermute(
            value, BOTH,
            self.pairs(lambda z, y, x, c: (z, y ^ 1, x, c) if c else (z, y, x ^ 1, c)),
        )

    def third(self, value):
        return lax.ppermute(
            value, BOTH,
            self.pairs(lambda z, y, x, c: (z, y, x ^ 1, c) if c else (z, y ^ 1, x, c)),
        )

    def core(self, value):
        return lax.ppermute(value, BOTH, self.pairs(lambda z, y, x, c: (z, y, x, c ^ 1)))

    def slots(self):
        z, y, x, c = self.spot()
        s = jnp.arange(self.dp * self.mp, dtype=jnp.int32)
        oz, oy, ox, oc = s >> 3, (s >> 2) & 1, (s >> 1) & 1, s & 1
        fx, fy = ox ^ x, oy ^ y
        early = jnp.where(oc == 0, fx, fy)
        late = jnp.where(oc == 0, fy, fx)
        return (oc ^ c) * 16 + late * 8 + early * 4 + (oz - z) % 4

    def gather(self, block):
        near = jnp.stack([block] + [self.along_z(block, 4 - k) for k in (1, 2, 3)])
        near = jnp.concatenate([near, self.second(near)])
        near = jnp.concatenate([near, self.third(near)])
        return jnp.concatenate([near, self.core(near)])

    def scatter(self, blocks):
        def add(a, b):
            return (a.astype(F32) + b.astype(F32)).astype(BF16)

        held = add(blocks[:16], self.core(blocks[16:]))
        held = add(held[:8], self.third(held[8:]))
        held = add(held[:4], self.second(held[4:]))
        total = held[0].astype(F32)
        for k in (1, 2, 3):
            total += self.along_z(held[k], k).astype(F32)
        return total

    def total(self, value):
        for move in (
            lambda z, y, x, c: (z, y, x, c ^ 1),
            lambda z, y, x, c: (z, y, x ^ 1, c),
            lambda z, y, x, c: (z, y ^ 1, x, c),
            lambda z, y, x, c: (z ^ 1, y, x, c),
            lambda z, y, x, c: (z ^ 2, y, x, c),
        ):
            value = value + lax.ppermute(value, BOTH, self.pairs(move))
        return value


def whole_of(grid, block, slots):
    lead, (rows, cols) = block.shape[:-2], block.shape[-2:]
    if not grid.fast:
        half = lax.all_gather(block, "dp", axis=len(lead), tiled=True)
        return lax.all_gather(half, "mp", axis=len(lead) + 1, tiled=True)
    pieces = jnp.take(grid.gather(block), slots, axis=0)
    pieces = pieces.reshape((grid.dp, grid.mp) + lead + (rows, cols))
    m = len(lead)
    order = tuple(range(2, 2 + m)) + (0, 2 + m, 1, 3 + m)
    return pieces.transpose(order).reshape(lead + (grid.dp * rows, grid.mp * cols))


def share_of(grid, whole, slots):
    lead, (rows, cols) = whole.shape[:-2], whole.shape[-2:]
    m = len(lead)
    if not grid.fast:
        half = lax.psum_scatter(whole, "mp", scatter_dimension=m + 1, tiled=True)
        return lax.psum_scatter(half, "dp", scatter_dimension=m, tiled=True).astype(F32)
    blocks = whole.reshape(lead + (grid.dp, rows // grid.dp, grid.mp, cols // grid.mp))
    order = (m, m + 2) + tuple(range(m)) + (m + 1, m + 3)
    blocks = blocks.transpose(order)
    blocks = blocks.reshape((grid.dp * grid.mp,) + blocks.shape[2:])
    back = jnp.zeros_like(slots).at[slots].set(jnp.arange(slots.shape[0], dtype=jnp.int32))
    return grid.scatter(jnp.take(blocks, back, axis=0))


def adam_update(
    weight, gradient, moment, square, average, step_rate, decay_rate, factor, step_count
):
    gradient = gradient * factor
    moment = beta_one * moment + (1.0 - beta_one) * gradient
    square = beta_two * square + (1.0 - beta_two) * gradient * gradient
    fixed_one = 1.0 - jnp.power(beta_one, step_count)
    fixed_two = 1.0 - jnp.power(beta_two, step_count)
    weight = weight - step_rate * (
        moment / fixed_one / (jnp.sqrt(square / fixed_two) + adam_eps) + decay_rate * weight
    )
    average = ema_decay * average + (1.0 - ema_decay) * weight
    return (weight, moment, square, average)


def per_device(
    grid,
    tokens,
    cotangent,
    clip_ids,
    frame_ids,
    step,
    w_qkv,
    w_out,
    w_up,
    w_down,
    norm_params,
    moment_qkv,
    moment_out,
    moment_up,
    moment_down,
    moment_norm,
    square_qkv,
    square_out,
    square_up,
    square_down,
    square_norm,
    average_qkv,
    average_out,
    average_up,
    average_down,
    average_norm,
):
    n, d = tokens.shape
    back_steps = CLIP // n
    mp_index = lax.axis_index("mp")
    slots = grid.slots() if grid.fast else None

    def shifted(value, k):
        pairs = [(i, i + k) for i in range(grid.mp) if 0 <= i + k < grid.mp]
        return lax.ppermute(value, "mp", pairs)

    halo = jnp.concatenate([shifted(tokens, k) for k in range(back_steps, 0, -1)])
    full_qkv = whole_of(grid, w_qkv.astype(BF16), slots)
    full_out = whole_of(grid, w_out.T.astype(BF16), slots)
    full_up = whole_of(grid, w_up.astype(BF16), slots)
    full_down = whole_of(grid, w_down.T.astype(BF16), slots)

    frames = lax.dynamic_slice_in_dim(frame_ids, mp_index * n, n, 0)
    low = (CLIP + jnp.arange(n, dtype=jnp.int32)) // FRAME - frames
    first = low[::TQ] * FRAME // TK
    low = low.reshape(1, n)

    q, k, v, kt, vt, xn = project(tokens, halo, norm_params, full_qkv)
    mixture, logs = attend(first, low, q, k, vt)
    block_out, gmix, gmid, gmid_low, n2, act, gh, gains_two = feed(
        tokens, mixture, cotangent, norm_params, full_out, full_up, full_down
    )
    gup, gdown, gout = feed_weights(n2, gh, cotangent, act, gmid_low, mixture)
    grad_up = share_of(grid, gup, slots)
    grad_down = share_of(grid, gdown, slots)
    grad_out = share_of(grid, gout, slots)
    dq, dk, dv = attend_back(first, low, q, k, v, kt, mixture, logs, gmix)
    grad_qkv = share_of(grid, project_weights(xn, dq, dk, dv), slots)
    grad_rows, back, gains_one = first_back(
        tokens, halo, norm_params, full_qkv, dq, dk, dv, gmid
    )
    grad_tokens = grad_rows
    for i, hop in enumerate(range(back_steps, 0, -1)):
        grad_tokens = grad_tokens + shifted(back[i * n : (i + 1) * n], -hop).astype(F32)

    def total(value):
        return grid.total(value) if grid.fast else lax.psum(value, BOTH)

    gain_grads = total(jnp.concatenate([gains_one, gains_two]))
    weight_square = (
        jnp.sum(grad_qkv * grad_qkv)
        + jnp.sum(grad_out * grad_out)
        + jnp.sum(grad_up * grad_up)
        + jnp.sum(grad_down * grad_down)
    )
    square_sum = total(jnp.broadcast_to(weight_square, (8, 128)))[0, 0] + jnp.sum(
        gain_grads * gain_grads
    )
    norm_value = jnp.sqrt(square_sum)
    factor = jnp.minimum(1.0, clip_limit / (norm_value + 1e-06))
    step_count = step[0].astype(F32)
    one = adam_update(
        w_qkv, grad_qkv, moment_qkv, square_qkv, average_qkv, 0.03, 0.1, factor, step_count
    )
    two = adam_update(
        w_out, grad_out.T, moment_out, square_out, average_out, 0.09, 0.1, factor, step_count
    )
    three = adam_update(
        w_up, grad_up, moment_up, square_up, average_up, 0.03, 0.1, factor, step_count
    )
    four = adam_update(
        w_down, grad_down.T, moment_down, square_down, average_down, 0.015, 0.1, factor, step_count
    )
    five = adam_update(
        norm_params,
        gain_grads,
        moment_norm,
        square_norm,
        average_norm,
        0.2,
        0.0,
        factor,
        step_count,
    )
    sets = (one, two, three, four, five)
    return (
        (block_out, grad_tokens, norm_value)
        + tuple(s[0] for s in sets)
        + tuple(s[1] for s in sets)
        + tuple(s[2] for s in sets)
        + tuple(s[0].astype(BF16) for s in sets[:4])
        + tuple(s[3] for s in sets)
    )


def solution(mesh):
    rows = P(BOTH, None)
    weights = (P(None, "dp", "mp"), P("mp", "dp"), P("dp", "mp"), P("mp", "dp"))
    states = weights + (P(),)
    return jax.shard_map(
        functools.partial(per_device, Grid(mesh.shape["dp"], mesh.shape["mp"])),
        mesh=mesh,
        in_specs=(rows, rows, P("dp"), P("dp"), P()) + states * 4,
        out_specs=(rows, rows, P()) + states * 3 + weights + states,
        check_vma=False,
    )
```

time: 1090 us -> 391 us (0.36)
  waiting for transfers between devices: 303 us -> 39.1 us
  matrix products: 232 us -> 0 us
  blocking collectives: 213 us -> 0 us
  Pallas kernels: 0 us -> 127 us
  other arithmetic: 140 us -> 33.5 us
  starting transfers between devices: 1.2 us -> 101 us
  local copies, waits for them, and re-layouts: 141 us -> 80.1 us
  loops' own time: 27.2 us -> 0 us
  between operations: 21.7 us -> 7.91 us
    dot_general x40 -> x0, matrix products: 232 us -> none  [the longest x8 69.3 us: window(): jnp.einsum('qhe,khe->hqk', query_block, key_block, preferred_element_type...]
    reduce_scatter x7 -> x0, waiting for transfers between devices: 210 us -> none  [the longest x1 44.3 us: per_device(): lax.psum_scatter(jnp.dot(piece, full_out, preferred_element_type=jnp.floa...]
    all_gather x4 -> x0, blocking collectives: 132 us -> none  [the longest x1 34.3 us: per_device(): lax.all_gather(w_out.astype(jnp.bfloat16), 'dp', axis=1, tiled=True)]
    pallas_call x0 -> x7, Pallas kernels: none -> 127 us  [call(): pl.pallas_call(body, out_shape=outs, in_specs=[pl.BlockSpec(memory_space=...]
    ppermute x0 -> x60, starting transfers between devices: none -> 101 us  [the longest x24 42.3 us: along_z(): lax.ppermute(value, BOTH, self.pairs(lambda z, y, x, c: ((z + k) % 4, y,...]
    psum x2 -> x0, blocking collectives: 80.6 us -> none  [the longest x1 41 us: per_device(): lax.psum(weight_square + jnp.where(leader, gain_square, 0.0), ('dp', 'mp'))]
    unnamed x13 -> x0, waiting for transfers between devices: 74.8 us -> none
    dynamic_slice x76 -> x0, local copies, waits for them, and re-layouts: 51 us -> none  [the longest x4 10.5 us: window(): lax.dynamic_slice_in_dim(pad_values, offset, window_rows, 0)]
  transfers between devices with their start and end apart: 12 -> 60, of which waited for: 7 -> 19; matrix products, arithmetic and copies ran while one was open for 32% -> 22% of each run, Pallas kernels for 0% -> 15%
where the time goes in v1:
time: 391 us; the launch traced here: 389 us
  Pallas kernels  127 us (32%)
  starting transfers between devices  101 us (26%)
  local copies, waits for them, and re-layouts  80.1 us (20%)
  waiting for transfers between devices  39.1 us (10%)
  other arithmetic  33.5 us (9%)
  between operations  7.91 us (2%)
    pallas_call x7, Pallas kernels, call(): pl.pallas_call(body, out_shape=outs, in_specs=[pl.BlockSpec(memory_space=...  127 us
    ppermute x24, starting transfers between devices, along_z(): lax.ppermute(value, BOTH, self.pairs(lambda z, y, x, c: ((z + k) % 4, y,...  42.3 us
    ppermute x8, starting transfers between devices, core(): lax.ppermute(value, BOTH, self.pairs(lambda z, y, x, c: (z, y, x, c ^ 1)))  21.6 us
    reshape x8, local copies, waits for them, and re-layouts, share_of(): whole.reshape(lead + (grid.dp, rows // grid.dp, grid.mp, cols // grid.mp))  21.5 us
    unnamed x109, local copies, waits for them, and re-layouts  19.5 us
    ppermute x8, waiting for transfers between devices, second(): lax.ppermute(value, BOTH, self.pairs(lambda z, y, x, c: (z, y ^ 1, x, c)...  16.7 us
    ppermute x8, starting transfers between devices, second(): lax.ppermute(value, BOTH, self.pairs(lambda z, y, x, c: (z, y ^ 1, x, c)...  11.8 us
    ppermute x10, starting transfers between devices, total(): value = value + lax.ppermute(value, BOTH, self.pairs(move))  11 us
  transfers between devices with their start and end apart: 60, of which 19 were waited for; matrix products, arithmetic and copies ran while one was open for 22% of the time, Pallas kernels for 15%

profile of v1, /device:TPU:0, one launch (start us, length us, event | category | flops | bytes accessed | tf_op | source)
XLA Modules:
  0.0 388.8 jit_solution(7116582706893033863)
XLA Ops:
  2.2 5.0 %collective-permute-start.13 = (bf16[64,512]{1,0:T(8,128)(2,1)S(1)}, bf16[64,512]{1,0:T(8,128)(2,1)S(1)}, u32[]{:S(2)}, u32[]{:S(2)}) collective-permute-start(bf16[64,512]{1,0:T(8,128)(2,1)S(1)} %get-tuple-element.105), channel_id=1, source_target_pairs={{0,24},{1,25},{2,26},{3,27},{4,28},{5,29},{6,30},{7,31},{8,0},{9,1... | collective-permute-start | bytes 196616 | tf_op jit(solution)/shard_map/ppermute | solution.py:450
  23.0 3.8 collective-permute-start.1
  54.9 8.8 %collective-permute-start.12 = (bf16[16,64,128]{2,1,0:T(8,128)(2,1)S(1)}, bf16[16,64,128]{2,1,0:T(8,128)(2,1)S(1)}, u32[]{:S(2)}, u32[]{:S(2)}) collective-permute-start(bf16[16,64,128]{2,1,0:T(8,128)(2,1)S(1)} %get-tuple-element.136), channel_id=1, source_target_pairs={{0,1},{1,0},{2,3},{3,2},{4,5},{5,4},{6,7},{7,6},{8,9},{9,8},{10,11... | collective-permute-start | bytes 786440 | tf_op jit(solution)/shard_map/ppermute | solution.py:465
  76.3 3.5 collective-permute-done.23
  91.2 12.2 %shard_map.439 = (bf16[1024,512]{1,0:T(8,128)(2,1)}, bf16[2048,512]{1,0:T(8,128)(2,1)}, bf16[2048,512]{1,0:T(8,128)(2,1)}, bf16[512,2048]{1,0:T(8,128)(2,1)}, bf...) custom-call(bf16[1024,512]{1,0:T(8,128)(2,1)} %own_ref.3, bf16[1024,512]{1,0:T(8,128)(2,1)} %collective-permute-done.halo_ref, ...), custom_call_target="tpu_custom_call" | custom-call | flops 2684354560 | bytes 15728640 | tf_op jit(solution)/shard_map/pallas_call | solution.py:44
  103.4 27.5 %shard_map.440 = (bf16[1024,512]{1,0:T(8,128)(2,1)}, f32[8,1024]{1,0:T(8,128)}) custom-call(s32[8]{0:T(128)} %and_select_fusion.2.first_ref, s32[1,1024]{1,0:T(1,128)} %bitcast.226, bf16[1024,512]{1,0:T(8,128)(2,1)} %get-tuple-element.55.q_ref, bf16[2048,512]{1,0:T(8,128)(2,1)} %get-tuple-element.56.k_ref, bf16[512,2048]{1,0:T(8,128)(2,1)} %get-tuple-element.57.vt_ref), custom_call_target="tpu_custom_call" | custom-call | flops 4294967296 | bytes 10485760 | tf_op jit(solution)/shard_map/pallas_call | solution.py:44
  136.5 3.6 gather_fusion.3
  149.3 24.6 %shard_map.441 = (bf16[1024,512]{1,0:T(8,128)(2,1)}, bf16[1024,512]{1,0:T(8,128)(2,1)}, f32[1024,512]{1,0:T(8,128)}, bf16[1024,512]{1,0:T(8,128)(2,1)}, bf16[102...) custom-call(bf16[1024,512]{1,0:T(8,128)(2,1)} %own_ref.3, ...), custom_call_target="tpu_custom_call" | custom-call | flops 9663676416 | bytes 22020096 | tf_op jit(solution)/shard_map/pallas_call | solution.py:44
  173.9 33.8 %shard_map.442 = (bf16[1024,512]{1,0:T(8,128)(2,1)}, bf16[2048,512]{1,0:T(8,128)(2,1)}, bf16[2048,512]{1,0:T(8,128)(2,1)}) custom-call(s32[8]{0:T(128)} %and_select_fusion.2.first_ref, s32[1,1024]{1,0:T(1,128)} %bitcast.227, bf16[1024,512]{1,0:T(8,128)(2,1)} %get-tuple-element.55.q_ref, bf16[2048,512]{1,0:T(8,128)(2,1)} %get-tuple-element.56.k_ref, ...), custom_call_target="tpu_custom_call" | custom-call | flops 10737418240 | bytes 14680064 | tf_op jit(solution)/shard_map/pallas_call | solution.py:44
  207.7 11.2 %shard_map.443 = (f32[1024,512]{1,0:T(8,128)}, bf16[1024,512]{1,0:T(8,128)(2,1)}, f32[2,512]{1,0:T(2,128)}) custom-call(bf16[1024,512]{1,0:T(8,128)(2,1)} %own_ref.3, bf16[1024,512]{1,0:T(8,128)(2,1)} %collective-permute-done.halo_ref, f32[4,512]{1,0:T(4,128)} %norm_ref.5, bf16[3,512,512]{2,1,0:T(8,128)(2,1)} %reshape.251.w_ref, ...), custom_call_target="tpu_custom_call" | custom-call | flops 2684354560 | bytes 14680064 | tf_op jit(solution)/shard_map/pallas_call | solution.py:44
  219.6 10.7 %shard_map.445 = (bf16[512,2048]{1,0:T(8,128)(2,1)}, bf16[512,2048]{1,0:T(8,128)(2,1)}, bf16[512,512]{1,0:T(8,128)(2,1)}) custom-call(bf16[1024,512]{1,0:T(8,128)(2,1)} %get-tuple-element.71.n2_ref, bf16[1024,2048]{1,0:T(8,128)(2,1)} %get-tuple-element.72.gh_ref, bf16[1024,512]{1,0:T(8,128)(2,1)} %cot_ref.3, bf16[1024,2048]{1,0:T(8,128)(2,1)} %get-tuple-element.73.act_ref, ...), custom_call_target="tpu_custom_call" | custom-call | flops 4831838208 | bytes 16777216 | tf_op jit(solution)/shard_map/pallas_call | solution.py:44
  230.3 4.5 %reshape.262 = bf16[8,64,4,512]{3,2,1,0:T(4,128)(2,1)} reshape(bf16[512,2048]{1,0:T(8,128)(2,1)} %get-tuple-element.76) | data formatting | bytes 4194304 | tf_op jit(solution)/shard_map/reshape | solution.py:524
  237.0 4.5 %reshape.264 = bf16[8,64,4,512]{3,2,1,0:T(4,128)(2,1)} reshape(bf16[512,2048]{1,0:T(8,128)(2,1)} %get-tuple-element.77) | data formatting | bytes 4194304 | tf_op jit(solution)/shard_map/reshape | solution.py:524
  241.4 3.4 copy.62
  252.6 7.3 %shard_map.444 = bf16[3,512,512]{2,1,0:T(8,128)(2,1)} custom-call(bf16[2048,512]{1,0:T(8,128)(2,1)} %get-tuple-element.70.xn_ref, bf16[1024,512]{1,0:T(8,128)(2,1)} %get-tuple-element.64.dq_ref, bf16[2048,512]{1,0:T(8,128)(2,1)} %get-tuple-element.65.dk_ref, bf16[2048,512]{1,0:T(8,128)(2,1)} %get-tuple-element.66.dv_ref), custom_call_target="tpu_custom_call" | custom-call | flops 2684354560 | bytes 8912896 | tf_op jit(solution)/shard_map/pallas_call | solution.py:44
  259.9 3.7 reshape.258
  263.6 3.0 copy.59
  266.6 3.3 gather_fusion.4
  273.9 9.6 %collective-permute-start.44 = (bf16[16,64,512]{2,1,0:T(8,128)(2,1)S(1)}, bf16[16,64,512]{2,1,0:T(8,128)(2,1)S(1)}, u32[]{:S(2)}, u32[]{:S(2)}) collective-permute-start(bf16[16,64,512]{2,1,0:T(8,128)(2,1)S(1)} %slice.215), channel_id=1, source_target_pairs={{0,1},{1,0},{2,3},{3,2},{4,5},{5,4},{6,7},{7,6},{8,9},{9,8},{10,11... | collective-permute-start | bytes 3145736 | tf_op jit(solution)/shard_map/ppermute | solution.py:465
  283.6 4.7 %collective-permute-start.34 = (bf16[4,64,128]{2,1,0:T(8,128)(2,1)S(1)}, bf16[4,64,128]{2,1,0:T(8,128)(2,1)S(1)}, u32[]{:S(2)}, u32[]{:S(2)}) collective-permute-start(bf16[4,64,128]{2,1,0:T(8,128)(2,1)S(1)} %slice.199), channel_id=1, source_target_pairs={{0,2},{1,5},{2,0},{3,7},{4,6},{5,1},{6,4},{7,3},{8,10},{9,13},{10,... | collective-permute-start | bytes 196616 | tf_op jit(solution)/shard_map/ppermute | solution.py:453
  295.8 10.7 %collective-permute-start.36 = (bf16[64,128]{1,0:T(8,128)(2,1)S(1)}, bf16[64,128]{1,0:T(8,128)(2,1)S(1)}, u32[]{:S(2)}, u32[]{:S(2)}) collective-permute-start(bf16[64,128]{1,0:T(8,128)(2,1)S(1)} %get-tuple-element.140), channel_id=1, source_target_pairs={{0,16},{1,17},{2,18},{3,19},{4,20},{5,21},{6,22},{7,23},{8,24},{9,... | collective-permute-start | bytes 49160 | tf_op jit(solution)/shard_map/ppermute | solution.py:450
  309.8 6.0 %collective-permute-done.28 = bf16[4,3,64,128]{3,2,1,0:T(8,128)(2,1)S(1)} collective-permute-done((bf16[4,3,64,128]{3,2,1,0:T(8,128)(2,1)S(1)}, bf16[4,3,64,128]{3,2,1,0:T(8,128)(2,1)S(1)}, u32[]{:S(2)}, u32[]{:S(2)}) %collective-permute-start.28) | collective-permute-done | bytes 196640 | tf_op jit(solution)/shard_map/ppermute | solution.py:453
  331.7 10.6 %collective-permute-done.46 = bf16[4,64,512]{2,1,0:T(8,128)(2,1)S(1)} collective-permute-done((bf16[4,64,512]{2,1,0:T(8,128)(2,1)S(1)}, bf16[4,64,512]{2,1,0:T(8,128)(2,1)S(1)}, u32[]{:S(2)}, u32[]{:S(2)}) %collective-permute-start.46) | collective-permute-done | bytes 262176 | tf_op jit(solution)/shard_map/ppermute | solution.py:453
  350.3 3.0 collective-permute-start.43
  (323 shorter events, 162.0 us)
Async XLA Ops:
  2.2 34.3 %collective-permute-start.13 = (bf16[64,512]{1,0:T(8,128)(2,1)S(1)}, bf16[64,512]{1,0:T(8,128)(2,1)S(1)}, u32[]{:S(2)}, u32[]{:S(2)}) collective-permute-start(bf16[64,512]{1,0:T(8,128)(2,1)S(1)} %get-tuple-element.105), channel_id=1, source_target_pairs={{0,24},{1,25},{2,26},{3,27},{4,28},{5,29},{6,30},{7,31},{8,0},{9,1... | collective-permute-start | bytes 196616 | tf_op jit(solution)/shard_map/ppermute | solution.py:450
  7.2 31.0 %collective-permute-start.14 = (bf16[64,512]{1,0:T(8,128)(2,1)S(1)}, bf16[64,512]{1,0:T(8,128)(2,1)S(1)}, u32[]{:S(2)}, u32[]{:S(2)}) collective-permute-start(bf16[64,512]{1,0:T(8,128)(2,1)S(1)} %get-tuple-element.105), channel_id=1, source_target_pairs={{0,16},{1,17},{2,18},{3,19},{4,20},{5,21},{6,22},{7,23},{8,24},{9,... | collective-permute-start | bytes 196616 | tf_op jit(solution)/shard_map/ppermute | solution.py:450
  7.2 33.4 %collective-permute-start.15 = (bf16[64,512]{1,0:T(8,128)(2,1)S(1)}, bf16[64,512]{1,0:T(8,128)(2,1)S(1)}, u32[]{:S(2)}, u32[]{:S(2)}) collective-permute-start(bf16[64,512]{1,0:T(8,128)(2,1)S(1)} %get-tuple-element.105), channel_id=1, source_target_pairs={{0,8},{1,9},{2,10},{3,11},{4,12},{5,13},{6,14},{7,15},{8,16},{9,17... | collective-permute-start | bytes 196616 | tf_op jit(solution)/shard_map/ppermute | solution.py:450
  38.3 52.9 %collective-permute-start = (bf16[1024,512]{1,0:T(8,128)(2,1)}, bf16[1024,512]{1,0:T(8,128)(2,1)}, u32[]{:S(2)}, u32[]{:S(2)}) collective-permute-start(bf16[1024,512]{1,0:T(8,128)(2,1)} %own_ref.3), channel_id=1, source_target_pairs={{0,1},{1,2},{2,3},{4,5},{5,6},{6,7},{8,9},{9,10},{10,11},{12,13},{... | collective-permute-start | bytes 3145736 | tf_op jit(solution)/shard_map/ppermute | solution.py:582
  42.8 20.9 %collective-permute-start.16 = (bf16[4,64,512]{2,1,0:T(8,128)(2,1)S(1)}, bf16[4,64,512]{2,1,0:T(8,128)(2,1)S(1)}, u32[]{:S(2)}, u32[]{:S(2)}) collective-permute-start(bf16[4,64,512]{2,1,0:T(8,128)(2,1)S(1)} %pad_maximum_fusion), channel_id=1, source_target_pairs={{0,2},{1,5},{2,0},{3,7},{4,6},{5,1},{6,4},{7,3},{8,10},{9,13},{10,... | collective-permute-start | bytes 786440 | tf_op jit(solution)/shard_map/ppermute | solution.py:453
  43.9 24.9 %collective-permute-start.22 = (bf16[4,64,512]{2,1,0:T(8,128)(2,1)S(1)}, bf16[4,64,512]{2,1,0:T(8,128)(2,1)S(1)}, u32[]{:S(2)}, u32[]{:S(2)}) collective-permute-start(bf16[4,64,512]{2,1,0:T(8,128)(2,1)S(1)} %pad_maximum_fusion.1), channel_id=1, source_target_pairs={{0,2},{1,5},{2,0},{3,7},{4,6},{5,1},{6,4},{7,3},{8,10},{9,13},{10,... | collective-permute-start | bytes 786440 | tf_op jit(solution)/shard_map/ppermute | solution.py:453
  50.8 15.4 %collective-permute-start.5 = (bf16[8,3,64,128]{3,2,1,0:T(8,128)(2,1)S(1)}, bf16[8,3,64,128]{3,2,1,0:T(8,128)(2,1)S(1)}, u32[]{:S(2)}, u32[]{:S(2)}) collective-permute-start(bf16[8,3,64,128]{3,2,1,0:T(8,128)(2,1)S(1)} %get-tuple-element.135), channel_id=1, source_target_pairs={{0,4},{1,3},{2,6},{3,1},{4,0},{5,7},{6,2},{7,5},{8,12},{9,11},{10,... | collective-permute-start | bytes 1179656 | tf_op jit(solution)/shard_map/ppermute | solution.py:459
  54.9 16.3 %collective-permute-start.12 = (bf16[16,64,128]{2,1,0:T(8,128)(2,1)S(1)}, bf16[16,64,128]{2,1,0:T(8,128)(2,1)S(1)}, u32[]{:S(2)}, u32[]{:S(2)}) collective-permute-start(bf16[16,64,128]{2,1,0:T(8,128)(2,1)S(1)} %get-tuple-element.136), channel_id=1, source_target_pairs={{0,1},{1,0},{2,3},{3,2},{4,5},{5,4},{6,7},{7,6},{8,9},{9,8},{10,11... | collective-permute-start | bytes 786440 | tf_op jit(solution)/shard_map/ppermute | solution.py:465
  67.3 14.5 %collective-permute-start.6 = (bf16[16,3,64,128]{3,2,1,0:T(8,128)(2,1)}, bf16[16,3,64,128]{3,2,1,0:T(8,128)(2,1)}, u32[]{:S(2)}, u32[]{:S(2)}) collective-permute-start(bf16[16,3,64,128]{3,2,1,0:T(8,128)(2,1)} %get-tuple-element.116), channel_id=1, source_target_pairs={{0,1},{1,0},{2,3},{3,2},{4,5},{5,4},{6,7},{7,6},{8,9},{9,8},{10,11... | collective-permute-start | bytes 2359304 | tf_op jit(solution)/shard_map/ppermute | solution.py:465
  76.3 54.5 %collective-permute-start.18 = (bf16[16,64,512]{2,1,0:T(8,128)(2,1)}, bf16[16,64,512]{2,1,0:T(8,128)(2,1)S(1)}, u32[]{:S(2)}, u32[]{:S(2)}) collective-permute-start(bf16[16,64,512]{2,1,0:T(8,128)(2,1)} %get-tuple-element.114), channel_id=1, source_target_pairs={{0,1},{1,0},{2,3},{3,2},{4,5},{5,4},{6,7},{7,6},{8,9},{9,8},{10,11... | collective-permute-start | bytes 3145736 | tf_op jit(solution)/shard_map/ppermute | solution.py:465
  81.7 52.5 %collective-permute-start.24 = (bf16[16,64,512]{2,1,0:T(8,128)(2,1)}, bf16[16,64,512]{2,1,0:T(8,128)(2,1)}, u32[]{:S(2)}, u32[]{:S(2)}) collective-permute-start(bf16[16,64,512]{2,1,0:T(8,128)(2,1)} %get-tuple-element.112), channel_id=1, source_target_pairs={{0,1},{1,0},{2,3},{3,2},{4,5},{5,4},{6,7},{7,6},{8,9},{9,8},{10,11... | collective-permute-start | bytes 3145736 | tf_op jit(solution)/shard_map/ppermute | solution.py:465
  219.6 68.7 %collective-permute-start.55 = (f32[4,512]{1,0:T(4,128)S(1)}, f32[4,512]{1,0:T(4,128)S(1)}, u32[]{:S(2)}, u32[]{:S(2)}) collective-permute-start(f32[4,512]{1,0:T(4,128)S(1)} %pad_maximum_fusion.4), channel_id=1, source_target_pairs={{0,1},{1,0},{2,3},{3,2},{4,5},{5,4},{6,7},{7,6},{8,9},{9,8},{10,11... | collective-permute-start | bytes 24584 | tf_op jit(solution)/shard_map/ppermute | solution.py:502
  252.0 19.7 %collective-permute-start.32 = (bf16[16,64,128]{2,1,0:T(8,128)(2,1)S(1)}, bf16[16,64,128]{2,1,0:T(8,128)(2,1)S(1)}, u32[]{:S(2)}, u32[]{:S(2)}) collective-permute-start(bf16[16,64,128]{2,1,0:T(8,128)(2,1)S(1)} %slice.195), channel_id=1, source_target_pairs={{0,1},{1,0},{2,3},{3,2},{4,5},{5,4},{6,7},{7,6},{8,9},{9,8},{10,11... | collective-permute-start | bytes 786440 | tf_op jit(solution)/shard_map/ppermute | solution.py:465
  271.6 21.0 %collective-permute-start.26 = (bf16[16,3,64,128]{3,2,1,0:T(8,128)(2,1)S(1)}, bf16[16,3,64,128]{3,2,1,0:T(8,128)(2,1)S(1)}, u32[]{:S(2)}, u32[]{:S(2)}) collective-permute-start(bf16[16,3,64,128]{3,2,1,0:T(8,128)(2,1)S(1)} %slice.185), channel_id=1, source_target_pairs={{0,1},{1,0},{2,3},{3,2},{4,5},{5,4},{6,7},{7,6},{8,9},{9,8},{10,11... | collective-permute-start | bytes 2359304 | tf_op jit(solution)/shard_map/ppermute | solution.py:465
  273.9 32.5 %collective-permute-start.44 = (bf16[16,64,512]{2,1,0:T(8,128)(2,1)S(1)}, bf16[16,64,512]{2,1,0:T(8,128)(2,1)S(1)}, u32[]{:S(2)}, u32[]{:S(2)}) collective-permute-start(bf16[16,64,512]{2,1,0:T(8,128)(2,1)S(1)} %slice.215), channel_id=1, source_target_pairs={{0,1},{1,0},{2,3},{3,2},{4,5},{5,4},{6,7},{7,6},{8,9},{9,8},{10,11... | collective-permute-start | bytes 3145736 | tf_op jit(solution)/shard_map/ppermute | solution.py:465
  288.5 19.4 %collective-permute-start.38 = (bf16[16,64,512]{2,1,0:T(8,128)(2,1)S(1)}, bf16[16,64,512]{2,1,0:T(8,128)(2,1)S(1)}, u32[]{:S(2)}, u32[]{:S(2)}) collective-permute-start(bf16[16,64,512]{2,1,0:T(8,128)(2,1)S(1)} %slice.205), channel_id=1, source_target_pairs={{0,1},{1,0},{2,3},{3,2},{4,5},{5,4},{6,7},{7,6},{8,9},{9,8},{10,11... | collective-permute-start | bytes 3145736 | tf_op jit(solution)/shard_map/ppermute | solution.py:465
  293.0 14.7 %collective-permute-start.27 = (bf16[8,3,64,128]{3,2,1,0:T(8,128)(2,1)S(1)}, bf16[8,3,64,128]{3,2,1,0:T(8,128)(2,1)S(1)}, u32[]{:S(2)}, u32[]{:S(2)}) collective-permute-start(bf16[8,3,64,128]{3,2,1,0:T(8,128)(2,1)S(1)} %slice.187), channel_id=1, source_target_pairs={{0,4},{1,3},{2,6},{3,1},{4,0},{5,7},{6,2},{7,5},{8,12},{9,11},{10,... | collective-permute-start | bytes 1179656 | tf_op jit(solution)/shard_map/ppermute | solution.py:459
  294.9 22.9 %collective-permute-start.35 = (bf16[64,128]{1,0:T(8,128)(2,1)S(1)}, bf16[64,128]{1,0:T(8,128)(2,1)S(1)}, u32[]{:S(2)}, u32[]{:S(2)}) collective-permute-start(bf16[64,128]{1,0:T(8,128)(2,1)S(1)} %get-tuple-element.138), channel_id=1, source_target_pairs={{0,8},{1,9},{2,10},{3,11},{4,12},{5,13},{6,14},{7,15},{8,16},{9,17... | collective-permute-start | bytes 49160 | tf_op jit(solution)/shard_map/ppermute | solution.py:450
  295.8 24.1 %collective-permute-start.36 = (bf16[64,128]{1,0:T(8,128)(2,1)S(1)}, bf16[64,128]{1,0:T(8,128)(2,1)S(1)}, u32[]{:S(2)}, u32[]{:S(2)}) collective-permute-start(bf16[64,128]{1,0:T(8,128)(2,1)S(1)} %get-tuple-element.140), channel_id=1, source_target_pairs={{0,16},{1,17},{2,18},{3,19},{4,20},{5,21},{6,22},{7,23},{8,24},{9,... | collective-permute-start | bytes 49160 | tf_op jit(solution)/shard_map/ppermute | solution.py:450
  306.5 16.0 %collective-permute-start.37 = (bf16[64,128]{1,0:T(8,128)(2,1)S(1)}, bf16[64,128]{1,0:T(8,128)(2,1)S(1)}, u32[]{:S(2)}, u32[]{:S(2)}) collective-permute-start(bf16[64,128]{1,0:T(8,128)(2,1)S(1)} %get-tuple-element.139), channel_id=1, source_target_pairs={{0,24},{1,25},{2,26},{3,27},{4,28},{5,29},{6,30},{7,31},{8,0},{9,1... | collective-permute-start | bytes 49160 | tf_op jit(solution)/shard_map/ppermute | solution.py:450
  307.7 21.4 %collective-permute-start.45 = (bf16[8,64,512]{2,1,0:T(8,128)(2,1)}, bf16[8,64,512]{2,1,0:T(8,128)(2,1)S(1)}, u32[]{:S(2)}, u32[]{:S(2)}) collective-permute-start(bf16[8,64,512]{2,1,0:T(8,128)(2,1)} %slice.217), channel_id=1, source_target_pairs={{0,4},{1,3},{2,6},{3,1},{4,0},{5,7},{6,2},{7,5},{8,12},{9,11},{10,... | collective-permute-start | bytes 1572872 | tf_op jit(solution)/shard_map/ppermute | solution.py:459
  315.8 15.6 %collective-permute-start.39 = (bf16[8,64,512]{2,1,0:T(8,128)(2,1)}, bf16[8,64,512]{2,1,0:T(8,128)(2,1)S(1)}, u32[]{:S(2)}, u32[]{:S(2)}) collective-permute-start(bf16[8,64,512]{2,1,0:T(8,128)(2,1)} %slice.207), channel_id=1, source_target_pairs={{0,4},{1,3},{2,6},{3,1},{4,0},{5,7},{6,2},{7,5},{8,12},{9,11},{10,... | collective-permute-start | bytes 1572872 | tf_op jit(solution)/shard_map/ppermute | solution.py:459
  324.0 49.6 %collective-permute-start.25 = (bf16[1024,512]{1,0:T(8,128)(2,1)}, bf16[1024,512]{1,0:T(8,128)(2,1)}, u32[]{:S(2)}, u32[]{:S(2)}) collective-permute-start(bf16[1024,512]{1,0:T(8,128)(2,1)} %get-tuple-element.69), channel_id=1, source_target_pairs={{1,0},{2,1},{3,2},{5,4},{6,5},{7,6},{9,8},{10,9},{11,10},{13,12},{... | collective-permute-start | bytes 3145736 | tf_op jit(solution)/shard_map/ppermute | solution.py:582
  325.3 32.8 %collective-permute-start.57 = (f32[4,512]{1,0:T(4,128)}, f32[4,512]{1,0:T(4,128)}, u32[]{:S(2)}, u32[]{:S(2)}) collective-permute-start(f32[4,512]{1,0:T(4,128)} %add.360), channel_id=1, source_target_pairs={{0,4},{1,5},{2,6},{3,7},{4,0},{5,1},{6,2},{7,3},{8,12},{9,13},{10,... | collective-permute-start | bytes 24584 | tf_op jit(solution)/shard_map/ppermute | solution.py:502
  (79 other events, 660.0 us)

commit v2 on v1

v2 whole, which is shorter than its diff:
```python
import functools

import jax
import jax.numpy as jnp
from jax import lax
from jax.experimental import pallas as pl
from jax.experimental.pallas import tpu as pltpu
from jax.sharding import PartitionSpec as P

HEAD = 64
CLIP = 1024
FRAME = 64

norm_eps = 1e-05
beta_one = 0.9
beta_two = 0.95
adam_eps = 1e-08
clip_limit = 1.0
ema_decay = 0.75

F32 = jnp.float32
BF16 = jnp.bfloat16
BOTH = ("dp", "mp")
VMEM = pltpu.VMEM
MASKED = -1e30
PAIR = 2 * HEAD
TQ = 256
TK = 256
ROWS = 256


def mm(a, b):
    return lax.dot_general(a, b, (((1,), (0,)), ((), ())), preferred_element_type=F32)


def mm_nt(a, b):
    return lax.dot_general(a, b, (((1,), (1,)), ((), ())), preferred_element_type=F32)


def mm_tn(a, b):
    return lax.dot_general(a, b, (((0,), (0,)), ((), ())), preferred_element_type=F32)


def shape(dims, kind):
    return jax.ShapeDtypeStruct(tuple(dims), kind)


def call(body, outs, smem, ins, far=(), scratch=(), flops=0, moved=0, room=60, loose=()):
    return pl.pallas_call(
        body,
        out_shape=outs,
        in_specs=[pl.BlockSpec(memory_space=pltpu.SMEM)] * len(smem)
        + [pl.BlockSpec(memory_space=VMEM)] * len(ins)
        + [pl.BlockSpec(memory_space=pl.ANY)] * len(far),
        out_specs=tuple(
            pl.BlockSpec(memory_space=pl.ANY if i in loose else VMEM) for i in range(len(outs))
        ),
        scratch_shapes=list(scratch),
        compiler_params=pltpu.CompilerParams(vmem_limit_bytes=room << 20),
        cost_estimate=pl.CostEstimate(
            flops=int(flops), bytes_accessed=int(moved), transcendentals=0
        ),
    )(*smem, *ins, *far)


def rows_at(tile, base=0):
    return pl.ds(pl.multiple_of(base + tile * ROWS, ROWS), ROWS)


def normalize(rows):
    center = rows - jnp.mean(rows, axis=-1, keepdims=True)
    inverse = lax.rsqrt(jnp.mean(center * center, axis=-1, keepdims=True) + norm_eps)
    return center * inverse, inverse


def norm_back(grad, xhat, inverse, gain_row):
    gy = grad * gain_row
    return inverse * (
        gy
        - jnp.mean(gy, axis=-1, keepdims=True)
        - xhat * jnp.mean(gy * xhat, axis=-1, keepdims=True)
    )


def place(spots_ref, far, sems, parts):
    copies = []
    for s in range(32):
        row, col = spots_ref[s] // 4, spots_ref[s] % 4
        for t, (start, wide, whole) in enumerate(parts):
            block = far[s // 4].at[s % 4]
            rows = block.shape[-2]
            at = (
                pl.ds(pl.multiple_of(row * rows, rows), rows),
                pl.ds(pl.multiple_of(col * wide, wide), wide),
            )
            lead = (slice(None),) * (len(block.shape) - 2)
            copies.append(
                pltpu.make_async_copy(
                    block.at[lead + (slice(None), pl.ds(start, wide))],
                    whole.at[lead + at],
                    sems.at[s * len(parts) + t],
                )
            )
    for copy in copies:
        copy.start()
    return copies


def project_body(fast, first_ref, *refs):
    if fast:
        spots_ref, own_ref, halo_ref, norm_ref = refs[:4]
        far, refs = refs[4:12], refs[12:]
        q_ref, k_ref, v_ref, vt_ref, w_ref, sems = refs
        for copy in place(spots_ref, far, sems, [(0, far[0].shape[-1], w_ref)]):
            copy.wait()
    else:
        own_ref, halo_ref, norm_ref, w_ref, q_ref, k_ref, v_ref, vt_ref = refs
    gain, shift = norm_ref[0:1, :], norm_ref[1:2, :]

    def rows_of(ref, tile, base, own):
        at, to = rows_at(tile), rows_at(tile, base)
        xhat, _ = normalize(ref[at, :].astype(F32))
        xn = (xhat * gain + shift).astype(BF16)
        if own:
            q = mm(xn, w_ref[0]).astype(BF16).astype(F32)
            q_ref[at, :] = (q * HEAD**-0.5).astype(BF16)
        k_ref[to, :] = mm(xn, w_ref[1]).astype(BF16)
        v = mm(xn, w_ref[2])
        v_ref[to, :] = v.astype(BF16)
        vt_ref[:, to] = v.T.astype(BF16)

    @pl.loop(jnp.minimum(first_ref[0], CLIP // ROWS), CLIP // ROWS)
    def _(tile):
        rows_of(halo_ref, tile, 0, False)

    @pl.loop(0, own_ref.shape[0] // ROWS)
    def _(tile):
        rows_of(own_ref, tile, CLIP, True)


def project(first, own, halo, norms, w_qkv, spots=None, far=()):
    n, d = own.shape
    total = n + CLIP
    fast = len(far) > 0
    outs = (
        shape((n, d), BF16),
        shape((total, d), BF16),
        shape((total, d), BF16),
        shape((d, total), BF16),
    )
    if fast:
        outs += (shape((3, d, d), BF16),)
    return call(
        functools.partial(project_body, fast),
        outs,
        (first, spots) if fast else (first,),
        (own, halo, norms) + (() if fast else (w_qkv,)),
        far,
        (pltpu.SemaphoreType.DMA((32,)),) if fast else (),
        flops=2 * d * d * (2 * total + n),
        moved=2 * d * (4 * total + 2 * n) + 6 * d * d,
        room=32,
    )


def split_heads(pair):
    lane = lax.broadcasted_iota(jnp.int32, pair.shape, 1)
    zero = jnp.zeros_like(pair)
    return jnp.concatenate([jnp.where(lane < HEAD, pair, zero), jnp.where(lane < HEAD, zero, pair)])


def twice(row):
    return jnp.concatenate([row, row], axis=1)


def sight(low_ref, at, i):
    spot = lax.broadcasted_iota(jnp.int32, (1, TQ), 1)
    last = ((CLIP + i * TQ) + spot) >> 6
    frame = lax.broadcasted_iota(jnp.int32, (TK, 2 * TQ), 0) >> 6
    return twice(low_ref[0:1, at]), twice(last), frame


def attend_body(
    first_ref, low_ref, q_ref, k_ref, vt_ref, mix_ref, log_ref, qt, acc, top, total, s_ref, p_ref
):
    pairs = q_ref.shape[1] // PAIR

    @pl.loop(0, q_ref.shape[0] // TQ)
    def _(i):
        at = pl.ds(pl.multiple_of(i * TQ, TQ), TQ)
        low, last, frame = sight(low_ref, at, i)
        for p in range(pairs):
            qt[p] = split_heads(q_ref[at, p * PAIR : (p + 1) * PAIR]).T
        acc[...] = jnp.zeros_like(acc)
        top[...] = jnp.full_like(top, MASKED)
        total[...] = jnp.zeros_like(total)

        def step(j, carry):
            keys = pl.ds(pl.multiple_of(j * TK, TK), TK)
            shift = j * (TK // FRAME)
            visible = (frame >= low - shift) & (frame <= last - shift)
            for p in range(pairs):
                scores = mm(k_ref[keys, p * PAIR : (p + 1) * PAIR], qt[p])
                s_ref[p] = jnp.where(visible, scores, MASKED)
            for p in range(pairs):
                scores = s_ref[p]
                old = top[p]
                new = jnp.maximum(old, jnp.max(scores, axis=0, keepdims=True))
                weights = jnp.exp(scores - new)
                keep = jnp.exp(old - new)
                top[p] = new
                total[p] = total[p] * keep + jnp.sum(weights, axis=0, keepdims=True)
                p_ref[p] = weights.astype(BF16)
                for h in range(2):
                    part = slice(h * HEAD, (h + 1) * HEAD)
                    acc[p, part, :] = acc[p, part, :] * keep[:, h * TQ : (h + 1) * TQ]
            for p in range(pairs):
                for h in range(2):
                    part = slice(h * HEAD, (h + 1) * HEAD)
                    values = vt_ref[p * PAIR + h * HEAD : p * PAIR + (h + 1) * HEAD, keys]
                    acc[p, part, :] += mm(values, p_ref[p, :, h * TQ : (h + 1) * TQ])
            return carry

        lax.fori_loop(first_ref[i], (CLIP + (i + 1) * TQ + TK - 1) // TK, step, 0)
        for p in range(pairs):
            sums = total[p]
            logs = top[p] + jnp.log(sums)
            inverse = 1.0 / sums
            for h in range(2):
                part = slice(h * HEAD, (h + 1) * HEAD)
                wide = slice(h * TQ, (h + 1) * TQ)
                acc[p, part, :] = acc[p, part, :] * inverse[:, wide]
                log_ref[2 * p + h : 2 * p + h + 1, at] = logs[:, wide]
            mix_ref[at, p * PAIR : (p + 1) * PAIR] = acc[p].T.astype(BF16)


def attend(first, low, q, k, vt):
    n, d = q.shape
    pairs = d // PAIR
    return call(
        attend_body,
        (shape((n, d), BF16), shape((d // HEAD, n), F32)),
        (first,),
        (low, q, k, vt),
        scratch=(
            VMEM((pairs, PAIR, 2 * TQ), BF16),
            VMEM((pairs, PAIR, TQ), F32),
            VMEM((pairs, 1, 2 * TQ), F32),
            VMEM((pairs, 1, 2 * TQ), F32),
            VMEM((pairs, TK, 2 * TQ), F32),
            VMEM((pairs, TK, 2 * TQ), BF16),
        ),
        flops=16 * n * 1024 * d,
        moved=2 * d * (2 * n + 2 * k.shape[0]),
        room=32,
    )


def put_blocks(slots_ref, m, grad, rows, put):
    for r in range(8):
        put(slots_ref[r * 4 + m] & 15, grad[r * rows : (r + 1) * rows])


def attend_back_body(fast, first_ref, *refs):
    if fast:
        slots_ref, side_ref, refs = refs[0], refs[1], refs[2:]
    (
        low_ref, q_ref, k_ref, v_ref, mix_ref, log_ref, grad_ref, own_ref, halo_ref, norm_ref,
        dq_ref, dk_ref, dv_ref,
    ) = refs[:13]
    outs, refs = refs[13 : 15 if fast else 14], refs[15 if fast else 14 :]
    kt_ref, xt_ref, qz, gz, qt, gt, acc, dk_acc, dv_acc, s_ref, d_ref, p_ref, ds_ref, rows_ref, g_acc = refs
    n, d = q_ref.shape
    pairs = d // PAIR
    start = first_ref[0]
    tiles = k_ref.shape[0] // ROWS
    gain, shift_row = norm_ref[0:1, :], norm_ref[1:2, :]

    def prepare(ref, tile, base):
        to = rows_at(tile, base)
        kt_ref[:, to] = k_ref[to, :].T
        xhat, _ = normalize(ref[rows_at(tile), :].astype(F32))
        xt_ref[:, to] = (xhat * gain + shift_row).T.astype(BF16)
        dk_acc[to, :] = jnp.zeros((ROWS, d), F32)
        dv_acc[to, :] = jnp.zeros((ROWS, d), F32)

    @pl.loop(jnp.minimum(start, CLIP // ROWS), CLIP // ROWS)
    def _(tile):
        prepare(halo_ref, tile, 0)

    @pl.loop(0, n // ROWS)
    def _(tile):
        prepare(own_ref, tile, CLIP)

    @pl.loop(0, n // TQ)
    def _(i):
        at = pl.ds(pl.multiple_of(i * TQ, TQ), TQ)
        low, last, frame = sight(low_ref, at, i)
        for p in range(pairs):
            lanes = slice(p * PAIR, (p + 1) * PAIR)
            grad = grad_ref[at, lanes]
            query_two, grad_two = split_heads(q_ref[at, lanes]), split_heads(grad)
            qz[p] = query_two
            gz[p] = grad_two
            qt[p] = query_two.T
            gt[p] = grad_two.T
            both = (grad.astype(F32) * mix_ref[at, lanes].astype(F32)).T
            for h in range(2):
                wide = slice(h * TQ, (h + 1) * TQ)
                rows_ref[p, 0:1, wide] = jnp.sum(
                    both[h * HEAD : (h + 1) * HEAD], axis=0, keepdims=True
                )
                rows_ref[p, 1:2, wide] = log_ref[2 * p + h : 2 * p + h + 1, at]
        acc[...] = jnp.zeros_like(acc)

        def step(j, carry):
            keys = pl.ds(pl.multiple_of(j * TK, TK), TK)
            shift = j * (TK // FRAME)
            visible = (frame >= low - shift) & (frame <= last - shift)
            for p in range(pairs):
                lanes = slice(p * PAIR, (p + 1) * PAIR)
                s_ref[p] = jnp.where(visible, mm(k_ref[keys, lanes], qt[p]), MASKED)
                d_ref[p] = mm(v_ref[keys, lanes], gt[p])
            for p in range(pairs):
                probs = jnp.exp(s_ref[p] - rows_ref[p, 1:2, :])
                p_ref[p] = probs.astype(BF16)
                ds_ref[p] = (probs * (d_ref[p] - rows_ref[p, 0:1, :])).astype(BF16)
            for p in range(pairs):
                lanes = slice(p * PAIR, (p + 1) * PAIR)
                dv_acc[keys, lanes] += mm(p_ref[p], gz[p])
                dk_acc[keys, lanes] += mm(ds_ref[p], qz[p])
                for h in range(2):
                    part = slice(h * HEAD, (h + 1) * HEAD)
                    rows = kt_ref[p * PAIR + h * HEAD : p * PAIR + (h + 1) * HEAD, keys]
                    acc[p, part, :] += mm(rows, ds_ref[p, :, h * TQ : (h + 1) * TQ])
            return carry

        lax.fori_loop(first_ref[i], (CLIP + (i + 1) * TQ + TK - 1) // TK, step, 0)
        for p in range(pairs):
            dq_ref[at, p * PAIR : (p + 1) * PAIR] = (acc[p].T * HEAD**-0.5).astype(BF16)

    @pl.loop(jnp.minimum(start, CLIP // ROWS), tiles)
    def _(tile):
        dk_ref[rows_at(tile), :] = dk_acc[rows_at(tile), :].astype(BF16)
        dv_ref[rows_at(tile), :] = dv_acc[rows_at(tile), :].astype(BF16)

    wide = g_acc.shape[2]

    def weights(m, put):
        cols = pl.ds(pl.multiple_of(m * wide, wide), wide)
        g_acc[0] = mm(xt_ref[:, CLIP:], dq_ref[:, cols])
        for s, grads in ((1, dk_ref), (2, dv_ref)):
            g_acc[s] = mm(xt_ref[:, CLIP:], grads[CLIP:, cols])

        @pl.loop(jnp.minimum(start, CLIP // ROWS), CLIP // ROWS)
        def _(tile):
            for s, grads in ((1, dk_ref), (2, dv_ref)):
                g_acc[s] += mm(xt_ref[:, rows_at(tile)], grads[rows_at(tile), cols])

        put(m)

    if not fast:
        for m in range(d // wide):

            def put(m):
                outs[0][:, :, m * wide : (m + 1) * wide] = g_acc[...].astype(BF16)

            weights(m, put)
        return
    rows = d // 8
    for side in range(2):
        for x in range(2):

            def put(m, out=outs[side]):
                for r in range(8):
                    slot = slots_ref[r * 4 + m] & 15
                    out[slot] = g_acc[:, r * rows : (r + 1) * rows, :].astype(BF16)

            weights(2 * x + side_ref[side], put)


def attend_back(first, low, q, k, v, mixture, logs, grad, own, halo, norms, slots=None, side=None):
    n, d = q.shape
    total = k.shape[0]
    pairs = d // PAIR
    fast = slots is not None
    outs = (shape((n, d), BF16), shape((total, d), BF16), shape((total, d), BF16))
    if fast:
        outs += (shape((16, 3, d // 8, d // 4), BF16),) * 2
    else:
        outs += (shape((3, d, d), BF16),)
    return call(
        functools.partial(attend_back_body, fast),
        outs,
        (first, slots, side) if fast else (first,),
        (low, q, k, v, mixture, logs, grad, own, halo, norms),
        scratch=(
            VMEM((d, total), BF16),
            VMEM((d, total), BF16),
            VMEM((pairs, 2 * TQ, PAIR), BF16),
            VMEM((pairs, 2 * TQ, PAIR), BF16),
            VMEM((pairs, PAIR, 2 * TQ), BF16),
            VMEM((pairs, PAIR, 2 * TQ), BF16),
            VMEM((pairs, PAIR, TQ), F32),
            VMEM((total, d), F32),
            VMEM((total, d), F32),
            VMEM((pairs, TK, 2 * TQ), F32),
            VMEM((pairs, TK, 2 * TQ), F32),
            VMEM((pairs, TK, 2 * TQ), BF16),
            VMEM((pairs, TK, 2 * TQ), BF16),
            VMEM((pairs, 8, 2 * TQ), F32),
            VMEM((3, d, d // 4), F32),
        ),
        flops=40 * n * 1024 * d,
        moved=2 * d * (4 * n + 4 * total),
        room=56,
    )


def feed_body(fast, *refs):
    if fast:
        spots_ref, slots_ref, side_ref, x_ref, mix_ref, cot_ref, norm_ref = refs[:7]
        far, refs = refs[7:15], refs[15:]
        out_ref, gmix_ref, gmid_ref, gain_ref = refs[:4]
        outs, refs = refs[4:6], refs[6:]
        wo_ref, up_ref, down_ref, sems = refs[:4]
        refs = refs[4:]
        one, ff = wo_ref.shape[1] // 4, up_ref.shape[1] // 4
        copies = place(
            spots_ref, far, sems,
            [(0, one, wo_ref), (one, ff, up_ref), (one + ff, ff, down_ref)],
        )
        for copy in copies:
            copy.wait()
    else:
        x_ref, mix_ref, cot_ref, norm_ref, wo_ref, up_ref, down_ref = refs[:7]
        out_ref, gmix_ref, gmid_ref, gain_ref = refs[7:11]
        outs, refs = refs[11:14], refs[14:]
    act_ref, gh_ref, n2t_ref, lowt_ref, cott_ref = refs
    gain, shift = norm_ref[2:3, :], norm_ref[3:4, :]
    ff = up_ref.shape[1]
    d = x_ref.shape[1]
    wide = min(512, ff)
    root = 0.7978845608028654
    gain_ref[...] = jnp.zeros_like(gain_ref)

    @pl.loop(0, x_ref.shape[0] // ROWS)
    def _(tile):
        at = rows_at(tile)
        cot = cot_ref[at, :]
        cott_ref[:, at] = cot.T
        middle = x_ref[at, :].astype(F32) + mm_nt(mix_ref[at, :], wo_ref[...])
        xhat, inverse = normalize(middle)
        n2 = xhat * gain + shift
        n2t_ref[:, at] = n2.T.astype(BF16)
        n2 = n2.astype(BF16)
        out = middle
        second = jnp.zeros_like(middle)
        for c in range(ff // wide):
            cols = slice(c * wide, (c + 1) * wide)
            hidden = mm(n2, up_ref[:, cols])
            square = hidden * hidden
            bent = jnp.tanh(hidden * (root + (root * 0.044715) * square))
            half = 0.5 + 0.5 * bent
            active = (hidden * half).astype(BF16)
            slope = half + hidden * (1.0 - bent * bent) * (
                0.5 * root + (0.5 * root * 3 * 0.044715) * square
            )
            act_ref[at, cols] = active
            out += mm_nt(active, down_ref[:, cols])
            gh = (mm(cot, down_ref[:, cols]) * slope).astype(BF16)
            gh_ref[at, cols] = gh
            second += mm_nt(gh, up_ref[:, cols])
        out_ref[at, :] = out.astype(BF16)
        gain_ref[0:1, :] += jnp.sum(second * xhat, axis=0, keepdims=True)
        gain_ref[1:2, :] += jnp.sum(second, axis=0, keepdims=True)
        gmid = cot.astype(F32) + norm_back(second, xhat, inverse, gain)
        gmid_ref[at, :] = gmid
        lowt_ref[:, at] = gmid.T.astype(BF16)
        gmix_ref[at, :] = mm(gmid.astype(BF16), wo_ref[...]).astype(BF16)

    if not fast:
        gup_ref, gdown_ref, gout_ref = outs
        for c in range(ff // wide):
            cols = slice(c * wide, (c + 1) * wide)
            gup_ref[:, cols] = mm(n2t_ref[...], gh_ref[:, cols]).astype(BF16)
            gdown_ref[:, cols] = mm(cott_ref[...], act_ref[:, cols]).astype(BF16)
        gout_ref[...] = mm(lowt_ref[...], mix_ref[...]).astype(BF16)
        return
    one, wide, rows = d // 4, ff // 4, d // 8
    for side in range(2):
        for x in range(2):
            m = 2 * x + side_ref[side]
            cols = pl.ds(pl.multiple_of(m * wide, wide), wide)
            small = pl.ds(pl.multiple_of(m * one, one), one)
            spots = [slots_ref[r * 4 + m] & 15 for r in range(8)]
            for start, size, left, right in (
                (0, one, lowt_ref, mix_ref[:, small]),
                (one, wide, n2t_ref, gh_ref[:, cols]),
                (one + wide, wide, cott_ref, act_ref[:, cols]),
            ):
                grad = mm(left[...], right).astype(BF16)
                for r in range(8):
                    outs[side][spots[r], :, start : start + size] = grad[r * rows : (r + 1) * rows]


def feed(x, mixture, cot, norms, full, ff, spots=None, slots=None, side=None, far=()):
    n, d = x.shape
    fast = len(far) > 0
    outs = (shape((n, d), BF16), shape((n, d), BF16), shape((n, d), F32), shape((2, d), F32))
    if fast:
        outs += (shape((16, d // 8, d // 4 + ff // 2), BF16),) * 2
    else:
        outs += (shape((d, ff), BF16), shape((d, ff), BF16), shape((d, d), BF16))
    return call(
        functools.partial(feed_body, fast),
        outs,
        (spots, slots, side) if fast else (),
        (x, mixture, cot, norms) + (() if fast else tuple(full)),
        far,
        (
            (
                VMEM((d, d), BF16),
                VMEM((d, ff), BF16),
                VMEM((d, ff), BF16),
                pltpu.SemaphoreType.DMA((96,)),
            )
            if fast
            else ()
        )
        + (
            VMEM((n, ff), BF16),
            VMEM((n, ff), BF16),
            VMEM((d, n), BF16),
            VMEM((d, n), BF16),
            VMEM((d, n), BF16),
        ),
        flops=2 * n * d * (6 * ff + 3 * d),
        moved=2 * n * 6 * d + 8 * d * ff,
        room=56,
    )


def first_back_body(
    first_ref, own_ref, halo_ref, norm_ref, w_ref, gmid_ref, dq_ref, dk_ref, dv_ref,
    grad_ref, back_ref, gain_ref,
):
    gain = norm_ref[0:1, :]
    gain_ref[...] = jnp.zeros_like(gain_ref)
    start = jnp.minimum(first_ref[0], CLIP // ROWS)

    def rows_of(ref, tile, base, own):
        at, to = rows_at(tile), rows_at(tile, base)
        first = mm_nt(dk_ref[to, :], w_ref[1]) + mm_nt(dv_ref[to, :], w_ref[2])
        if own:
            first += mm_nt(dq_ref[at, :], w_ref[0])
        xhat, inverse = normalize(ref[at, :].astype(F32))
        gain_ref[0:1, :] += jnp.sum(first * xhat, axis=0, keepdims=True)
        gain_ref[1:2, :] += jnp.sum(first, axis=0, keepdims=True)
        grad = norm_back(first, xhat, inverse, gain)
        if own:
            grad_ref[at, :] = gmid_ref[at, :] + grad
        else:
            back_ref[at, :] = grad.astype(BF16)

    @pl.loop(0, start)
    def _(tile):
        back_ref[rows_at(tile), :] = jnp.zeros((ROWS, back_ref.shape[1]), BF16)

    @pl.loop(start, CLIP // ROWS)
    def _(tile):
        rows_of(halo_ref, tile, 0, False)

    @pl.loop(0, own_ref.shape[0] // ROWS)
    def _(tile):
        rows_of(own_ref, tile, CLIP, True)


def first_back(first, own, halo, norms, w_qkv, gmid, dq, dk, dv):
    n, d = own.shape
    total = n + CLIP
    return call(
        first_back_body,
        (shape((n, d), F32), shape((CLIP, d), BF16), shape((2, d), F32)),
        (first,),
        (own, halo, norms, w_qkv, gmid, dq, dk, dv),
        flops=2 * d * d * (2 * total + n),
        moved=2 * d * (4 * total + 6 * n),
        room=32,
    )


class Grid:
    def __init__(self, dp, mp):
        self.dp, self.mp = dp, mp
        self.fast = (dp, mp) == (8, 4)

    def swap(self, value, z=0, y=0, x=0, c=0, swapped=False):
        pairs = []
        for i in range(self.dp * self.mp):
            dy, dx = (x, y) if swapped and i & 1 else (y, x)
            pairs.append((i, i ^ (z * 8 + dy * 4 + dx * 2 + c)))
        return lax.ppermute(value, BOTH, pairs)

    def early(self, value):
        return self.swap(value, x=1, swapped=True)

    def late(self, value):
        return self.swap(value, y=1, swapped=True)

    def spot(self):
        dp, mp = lax.axis_index("dp"), lax.axis_index("mp")
        return dp // 2, dp % 2, mp // 2, mp % 2

    def slots(self):
        z, y, x, c = self.spot()
        s = jnp.arange(32, dtype=jnp.int32)
        oz, oy, ox, oc = s >> 3, (s >> 2) & 1, (s >> 1) & 1, s & 1
        fx, fy = ox ^ x, oy ^ y
        return (
            (oc ^ c) * 16
            + jnp.where(oc == 0, fy, fx) * 8
            + jnp.where(oc == 0, fx, fy) * 4
            + (oz ^ z)
        )

    def spots(self):
        z, y, x, c = self.spot()
        s = jnp.arange(32, dtype=jnp.int32)
        oc, late, early, oz = (s >> 4) ^ c, (s >> 3) & 1, (s >> 2) & 1, (s & 3) ^ z
        oy = y ^ jnp.where(oc == 0, late, early)
        ox = x ^ jnp.where(oc == 0, early, late)
        return ((oz * 2 + oy) * 2 + ox) * 2 + oc

    def sides(self):
        c = lax.axis_index("mp") % 2
        return jnp.stack([c, 1 - c]).astype(jnp.int32)

    def gather_z(self, block):
        return jnp.stack([block] + [self.swap(block, z=k) for k in (1, 2, 3)])

    def across(self, held):
        return tuple(self.swap(a, c=1) for a in held)

    def scatter_core(self, sent):
        return self.swap(sent, c=1)

    def scatter_late(self, kept, got):
        return added(kept[:8], got[:8]), self.late(added(kept[8:], got[8:]))

    def scatter_early(self, kept, got):
        return added(kept[:4], got[:4]), self.early(added(kept[4:], got[4:]))

    def scatter_z(self, kept, got):
        parts = [added(kept[k], got[k]) for k in range(4)]
        near = [parts[0]] + [self.swap(parts[k], z=k) for k in (1, 2, 3)]
        near = [a.astype(F32) for a in near]
        return (near[0] + near[1]) + (near[2] + near[3])

    def total(self, value):
        value = value + self.swap(value, c=1)
        x, y, xy = (self.swap(value, x=a, y=b) for a, b in ((1, 0), (0, 1), (1, 1)))
        value = (value + x) + (y + xy)
        one, two, three = (self.swap(value, z=k) for k in (1, 2, 3))
        return (value + one) + (two + three)


def added(a, b):
    return (a.astype(F32) + b.astype(F32)).astype(BF16)


def whole_of(block):
    m = block.ndim - 2
    half = lax.all_gather(block, "dp", axis=m, tiled=True)
    return lax.all_gather(half, "mp", axis=m + 1, tiled=True)


def share_of(whole):
    m = whole.ndim - 2
    half = lax.psum_scatter(whole, "mp", scatter_dimension=m + 1, tiled=True)
    return lax.psum_scatter(half, "dp", scatter_dimension=m, tiled=True).astype(F32)


def after(value, *others):
    return lax.optimization_barrier((value,) + others)[0]


def joined(*values):
    return lax.optimization_barrier(values)


def adam_update(
    weight, gradient, moment, square, average, step_rate, decay_rate, factor, step_count
):
    gradient = gradient * factor
    moment = beta_one * moment + (1.0 - beta_one) * gradient
    square = beta_two * square + (1.0 - beta_two) * gradient * gradient
    fixed_one = 1.0 - jnp.power(beta_one, step_count)
    fixed_two = 1.0 - jnp.power(beta_two, step_count)
    weight = weight - step_rate * (
        moment / fixed_one / (jnp.sqrt(square / fixed_two) + adam_eps) + decay_rate * weight
    )
    average = ema_decay * average + (1.0 - ema_decay) * weight
    return (weight, moment, square, average)


def per_device(
    grid,
    tokens,
    cotangent,
    clip_ids,
    frame_ids,
    step,
    w_qkv,
    w_out,
    w_up,
    w_down,
    norm_params,
    moment_qkv,
    moment_out,
    moment_up,
    moment_down,
    moment_norm,
    square_qkv,
    square_out,
    square_up,
    square_down,
    square_norm,
    average_qkv,
    average_out,
    average_up,
    average_down,
    average_norm,
):
    n, d = tokens.shape
    back_steps = CLIP // n
    mp_index = lax.axis_index("mp")

    def shifted(value, k):
        pairs = [(i, i + k) for i in range(grid.mp) if 0 <= i + k < grid.mp]
        return lax.ppermute(value, "mp", pairs)

    frames = lax.dynamic_slice_in_dim(frame_ids, mp_index * n, n, 0)
    low = (CLIP + jnp.arange(n, dtype=jnp.int32)) // FRAME - frames
    first = low[::TQ] * FRAME // TK
    low = low.reshape(1, n)

    low_qkv, low_out, low_up, low_down = (
        w_qkv.astype(BF16),
        w_out.T.astype(BF16),
        w_up.astype(BF16),
        w_down.T.astype(BF16),
    )
    if grid.fast:
        slots, spots, side = grid.slots(), grid.spots(), grid.sides()
        rest = jnp.concatenate([low_out, low_up, low_down], axis=1)
        near, halo = joined(grid.gather_z(low_qkv), shifted(tokens, 1))
        rest = after(rest, near)
        near_rest = grid.gather_z(rest)
        one, two = grid.early(near), grid.late(near)
        one, two = joined(one, two)
        held = (near, one, two, grid.late(one))
        near_rest, *held = joined(near_rest, *held)
        far = tuple(held) + grid.across(held)
        one, two = grid.early(near_rest), grid.late(near_rest)
        q, k, v, vt, full_qkv = project(first, tokens, halo, norm_params, None, spots, far)
        one, two, q = joined(one, two, q)
        three = grid.late(one)
        mixture, logs = attend(first, low, q, k, vt)
        three, mixture = joined(three, mixture)
        held = (near_rest, one, two, three)
        far = held + grid.across(held)
        block_out, gmix, gmid, gains_two, kept, sent = feed(
            tokens, mixture, cotangent, norm_params, None, 4 * low_up.shape[1], spots, slots, side, far
        )
        got = grid.scatter_core(sent)
        got, gmix = joined(got, gmix)
        kept, got = grid.scatter_late(kept, got)
        dq, dk, dv, kept_qkv, sent = attend_back(
            first, low, q, k, v, mixture, logs, gmix, tokens, halo, norm_params, slots, side
        )
        got, sent, dq = joined(got, sent, dq)
        got_qkv = grid.scatter_core(sent)
        kept, got = grid.scatter_early(kept, got)
        kept_qkv, got_qkv = grid.scatter_late(kept_qkv, got_qkv)
        grad_rows, back, gains_one = first_back(
            first, tokens, halo, norm_params, full_qkv, gmid, dq, dk, dv
        )
        got, got_qkv, back = joined(got, got_qkv, back)
        grad_rest = grid.scatter_z(kept, got)
        kept_qkv, got_qkv = grid.scatter_early(kept_qkv, got_qkv)
        grad_qkv = grid.scatter_z(kept_qkv, got_qkv)
        wide = d // 4
        grad_out, grad_up, grad_down = (
            grad_rest[:, :wide],
            grad_rest[:, wide : wide + low_up.shape[1]],
            grad_rest[:, wide + low_up.shape[1] :],
        )
    else:
        halo = jnp.concatenate([shifted(tokens, k) for k in range(back_steps, 0, -1)])
        full_qkv = whole_of(low_qkv)
        full = tuple(whole_of(a) for a in (low_out, low_up, low_down))
        q, k, v, vt = project(first, tokens, halo, norm_params, full_qkv)
        mixture, logs = attend(first, low, q, k, vt)
        block_out, gmix, gmid, gains_two, gup, gdown, gout = feed(
            tokens, mixture, cotangent, norm_params, full, full[1].shape[1]
        )
        grad_up, grad_down, grad_out = share_of(gup), share_of(gdown), share_of(gout)
        dq, dk, dv, gqkv = attend_back(
            first, low, q, k, v, mixture, logs, gmix, tokens, halo, norm_params
        )
        grad_qkv = share_of(gqkv)
        grad_rows, back, gains_one = first_back(
            first, tokens, halo, norm_params, full_qkv, gmid, dq, dk, dv
        )
    grad_tokens = grad_rows
    for i, hop in enumerate(range(back_steps, 0, -1)):
        grad_tokens = grad_tokens + shifted(back[i * n : (i + 1) * n], -hop).astype(F32)

    weight_square = (
        jnp.sum(grad_qkv * grad_qkv)
        + jnp.sum(grad_out * grad_out)
        + jnp.sum(grad_up * grad_up)
        + jnp.sum(grad_down * grad_down)
    )
    sums = jnp.concatenate(
        [gains_one, gains_two, jnp.broadcast_to(weight_square, (4, gains_one.shape[1]))]
    )
    sums = grid.total(sums) if grid.fast else lax.psum(sums, BOTH)
    gain_grads = sums[:4]
    norm_value = jnp.sqrt(sums[4, 0] + jnp.sum(gain_grads * gain_grads))
    factor = jnp.minimum(1.0, clip_limit / (norm_value + 1e-06))
    step_count = step[0].astype(F32)
    sets = (
        adam_update(
            w_qkv, grad_qkv, moment_qkv, square_qkv, average_qkv, 0.03, 0.1, factor, step_count
        ),
        adam_update(
            w_out, grad_out.T, moment_out, square_out, average_out, 0.09, 0.1, factor, step_count
        ),
        adam_update(
            w_up, grad_up, moment_up, square_up, average_up, 0.03, 0.1, factor, step_count
        ),
        adam_update(
            w_down, grad_down.T, moment_down, square_down, average_down, 0.015, 0.1, factor, step_count
        ),
        adam_update(
            norm_params, gain_grads, moment_norm, square_norm, average_norm, 0.2, 0.0, factor, step_count
        ),
    )
    return (
        (block_out, grad_tokens, norm_value)
        + tuple(s[0] for s in sets)
        + tuple(s[1] for s in sets)
        + tuple(s[2] for s in sets)
        + tuple(s[0].astype(BF16) for s in sets[:4])
        + tuple(s[3] for s in sets)
    )


def solution(mesh):
    rows = P(BOTH, None)
    weights = (P(None, "dp", "mp"), P("mp", "dp"), P("dp", "mp"), P("mp", "dp"))
    states = weights + (P(),)
    return jax.shard_map(
        functools.partial(per_device, Grid(mesh.shape["dp"], mesh.shape["mp"])),
        mesh=mesh,
        in_specs=(rows, rows, P("dp"), P("dp"), P()) + states * 4,
        out_specs=(rows, rows, P()) + states * 3 + weights + states,
        check_vma=False,
    )
```

time: 391 us -> 228 us (0.58)
  local copies, waits for them, and re-layouts: 80.1 us -> 7.35 us
  Pallas kernels: 127 us -> 83.2 us
  starting transfers between devices: 101 us -> 61.5 us
  other arithmetic: 33.5 us -> 26.9 us
    pallas_call x7 -> x5, Pallas kernels: 127 us -> 83.2 us  [call(): pl.pallas_call(body, out_shape=outs, in_specs=[pl.BlockSpec(memory_space=...]
    ppermute x58 -> x39, starting transfers between devices: 97.4 us -> 57.7 us  [swap(): return lax.ppermute(value, BOTH, pairs)]
    reshape x13 -> x0, local copies, waits for them, and re-layouts: 28.8 us -> none  [the longest x8 21.5 us: share_of(): whole.reshape(lead + (grid.dp, rows // grid.dp, grid.mp, cols // grid.mp))]
    gather x8 -> x0, local copies, waits for them, and re-layouts: 17.8 us -> none  [the longest x4 9.03 us: share_of(): return grid.scatter(jnp.take(blocks, back, axis=0))]
    unnamed x109 -> x80, local copies, waits for them, and re-layouts: 19.5 us -> 6.67 us
    concatenate x8 -> x1, local copies, waits for them, and re-layouts: 10.7 us -> 0.07 us  [per_device(): jnp.concatenate([gains_one, gains_two, jnp.broadcast_to(weight_square, (4...]
    unnamed x4 -> x0, other arithmetic: 5.97 us -> none
    select_n x8 -> x0, other arithmetic: 5.57 us -> none  [the longest x4 3.2 us: share_of(): return grid.scatter(jnp.take(blocks, back, axis=0))]
  transfers between devices with their start and end apart: 60 -> 41, of which waited for: 19 -> 20; matrix products, arithmetic and copies ran while one was open for 22% -> 9% of each run, Pallas kernels for 15% -> 23%
where the time goes in v2:
time: 228 us; the launch traced here: 227 us
  Pallas kernels  83.2 us (36%)
  starting transfers between devices  61.5 us (27%)
  waiting for transfers between devices  41.4 us (18%)
  other arithmetic  26.9 us (12%)
  local copies, waits for them, and re-layouts  7.35 us (3%)
  between operations  7.01 us (3%)
    pallas_call x5, Pallas kernels, call(): pl.pallas_call(body, out_shape=outs, in_specs=[pl.BlockSpec(memory_space=...  83.2 us
    ppermute x39, starting transfers between devices, swap(): return lax.ppermute(value, BOTH, pairs)  57.7 us
    ppermute x39, waiting for transfers between devices, swap(): return lax.ppermute(value, BOTH, pairs)  41.4 us
    add x5, other arithmetic, adam_update(): average = ema_decay * average + (1.0 - ema_decay) * weight  6.75 us
    unnamed x80, local copies, waits for them, and re-layouts  6.67 us
  transfers between devices with their start and end apart: 41, of which 20 were waited for; matrix products, arithmetic and copies ran while one was open for 9% of the time, Pallas kernels for 23%

profile of v2, /device:TPU:0, one launch (start us, length us, event | category | flops | bytes accessed | tf_op | source)
XLA Modules:
  0.0 227.5 jit_solution(5427953038742517678)
XLA Ops:
  0.7 2.6 %collective-permute-start.3 = (bf16[1024,512]{1,0:T(8,128)(2,1)}, bf16[1024,512]{1,0:T(8,128)(2,1)S(1)}, u32[]{:S(2)}, u32[]{:S(2)}) collective-permute-start(bf16[1024,512]{1,0:T(8,128)(2,1)} %own_ref.1), channel_id=1, source_target_pairs={{0,1},{1,2},{2,3},{4,5},{5,6},{6,7},{8,9},{9,10},{10,11},{12,13},{... | collective-permute-start | bytes 3145736 | tf_op jit(solution)/shard_map/ppermute | solution.py:741
  4.2 4.4 %collective-permute-start.2 = (bf16[3,64,128]{2,1,0:T(8,128)(2,1)S(1)}, bf16[3,64,128]{2,1,0:T(8,128)(2,1)S(1)}, u32[]{:S(2)}, u32[]{:S(2)}) collective-permute-start(bf16[3,64,128]{2,1,0:T(8,128)(2,1)S(1)} %convert_element_type.252), channel_id=1, source_target_pairs={{0,24},{1,25},{2,26},{3,27},{4,28},{5,29},{6,30},{7,31},{8,16},{9,... | collective-permute-start | bytes 147464 | tf_op jit(solution)/shard_map/ppermute | solution.py:603
  14.0 6.1 %collective-permute-start.7 = (bf16[4,3,64,128]{3,2,1,0:T(8,128)(2,1)S(1)}, bf16[4,3,64,128]{3,2,1,0:T(8,128)(2,1)S(1)}, u32[]{:S(2)}, u32[]{:S(2)}) collective-permute-start(bf16[4,3,64,128]{3,2,1,0:T(8,128)(2,1)S(1)} %pad_maximum_fusion.1.refs_4_), channel_id=1, source_target_pairs={{0,2},{1,5},{2,0},{3,7},{4,6},{5,1},{6,4},{7,3},{8,10},{9,13},{10,... | collective-permute-start | bytes 589832 | tf_op jit(solution)/shard_map/ppermute | solution.py:603
  21.6 3.7 %collective-permute-start.6 = (bf16[64,1152]{1,0:T(8,128)(2,1)S(1)}, bf16[64,1152]{1,0:T(8,128)(2,1)S(1)}, u32[]{:S(2)}, u32[]{:S(2)}) collective-permute-start(bf16[64,1152]{1,0:T(8,128)(2,1)S(1)} %pad_maximum_fusion.2), channel_id=1, source_target_pairs={{0,24},{1,25},{2,26},{3,27},{4,28},{5,29},{6,30},{7,31},{8,16},{9,... | collective-permute-start | bytes 442376 | tf_op jit(solution)/shard_map/ppermute | solution.py:603
  27.3 2.8 %collective-permute-done.6 = bf16[64,1152]{1,0:T(8,128)(2,1)S(1)} collective-permute-done((bf16[64,1152]{1,0:T(8,128)(2,1)S(1)}, bf16[64,1152]{1,0:T(8,128)(2,1)S(1)}, u32[]{:S(2)}, u32[]{:S(2)}) %collective-permute-start.6) | collective-permute-done | bytes 147488 | tf_op jit(solution)/shard_map/ppermute | solution.py:603
  30.1 5.3 %collective-permute-done.5 = bf16[64,1152]{1,0:T(8,128)(2,1)S(1)} collective-permute-done((bf16[64,1152]{1,0:T(8,128)(2,1)S(1)}, bf16[64,1152]{1,0:T(8,128)(2,1)S(1)}, u32[]{:S(2)}, u32[]{:S(2)}) %collective-permute-start.5) | collective-permute-done | bytes 147488 | tf_op jit(solution)/shard_map/ppermute | solution.py:603
  41.5 4.9 %shard_map.439 = (bf16[1024,512]{1,0:T(8,128)(2,1)S(1)}, bf16[2048,512]{1,0:T(8,128)(2,1)S(1)}, bf16[2048,512]{1,0:T(8,128)(2,1)S(1)}, bf16[512,2048]{1,0:T(8,128)(2,1)S(1)}, bf16[3,512,512]{2,1,0:T(8,128)(2,1)S(1)}) custom-call(s32[4]{0:T(128)S(1)} %and_select_fusion.first_ref, s32[32]{0:T(128)S(1)} %multiply_add_fusion.8.refs_0_, ...), custom_call_target="tpu_custom_call" | custom-call | flops 2684354560 | bytes 12058624 | tf_op jit(solution)/shard_map/pallas_call | solution.py:49
  47.7 5.7 %collective-permute-done.10.refs_8_ = bf16[4,64,1152]{2,1,0:T(8,128)(2,1)} collective-permute-done((bf16[4,64,1152]{2,1,0:T(8,128)(2,1)}, bf16[4,64,1152]{2,1,0:T(8,128)(2,1)}, u32[]{:S(2)}, u32[]{:S(2)}) %collective-permute-start.10) | collective-permute-done | bytes 589856 | tf_op jit(solution)/shard_map/ppermute | solution.py:603
  54.6 13.2 %shard_map.440 = (bf16[1024,512]{1,0:T(8,128)(2,1)S(1)}, f32[8,1024]{1,0:T(8,128)S(1)}) custom-call(s32[4]{0:T(128)S(1)} %and_select_fusion.first_ref, s32[1,1024]{1,0:T(1,128)S(1)} %bitcast.56, bf16[1024,512]{1,0:T(8,128)(2,1)S(1)} %get-tuple-element.83.q_ref.refs_3_, bf16[2048,512]{1,0:T(8,128)(2,1)S(1)} %get-tuple-element.84.k_ref.refs_4_, ...), custom_call_target="tpu_custom_call" | custom-call | flops 8589934592 | bytes 6291456 | tf_op jit(solution)/shard_map/pallas_call | solution.py:49
  72.4 30.6 %shard_map.441 = (bf16[1024,512]{1,0:T(8,128)(2,1)}, bf16[1024,512]{1,0:T(8,128)(2,1)}, f32[1024,512]{1,0:T(8,128)}, f32[2,512]{1,0:T(2,128)}, bf16[16,64,1152]{...) custom-call(s32[32]{0:T(128)} %copy-done.15, s32[32]{0:T(128)} %xor_add_fusion.refs_1_.refs_0_, ...), custom_call_target="tpu_custom_call" | custom-call | flops 14495514624 | bytes 14680064 | tf_op jit(solution)/shard_map/pallas_call | solution.py:49
  103.2 4.7 %collective-permute-done.21 = bf16[16,64,1152]{2,1,0:T(8,128)(2,1)S(1)} collective-permute-done((bf16[16,64,1152]{2,1,0:T(8,128)(2,1)}, bf16[16,64,1152]{2,1,0:T(8,128)(2,1)S(1)}, u32[]{:S(2)}, u32[]{:S(2)}) %collective-permute-start.21) | collective-permute-done | bytes 2359328 | tf_op jit(solution)/shard_map/ppermute | solution.py:603
  107.9 2.3 add_convert_fusion
  111.1 30.8 %shard_map.442 = (bf16[1024,512]{1,0:T(8,128)(2,1)}, bf16[2048,512]{1,0:T(8,128)(2,1)}, bf16[2048,512]{1,0:T(8,128)(2,1)}, bf16[16,3,64,128]{3,2,1,0:T(8,128)(2,1)}, bf16[16,3,64,128]{3,2,1,0:T(8,128)(2,1)}) custom-call(s32[4]{0:T(128)} %copy-done.13, s32[32]{0:T(128)} %xor_add_fusion.refs_1_.refs_0_, s32[2]{0:T(128)} %pad_add_fusion.refs_2_.refs_1_, ...), custom_call_target="tpu_custom_call" | custom-call | flops 21474836480 | bytes 12582912 | tf_op jit(solution)/shard_map/pallas_call | solution.py:49
  141.9 4.6 %collective-permute-start.24 = (bf16[16,3,64,128]{3,2,1,0:T(8,128)(2,1)}, bf16[16,3,64,128]{3,2,1,0:T(8,128)(2,1)S(1)}, u32[]{:S(2)}, u32[]{:S(2)}) collective-permute-start(bf16[16,3,64,128]{3,2,1,0:T(8,128)(2,1)} %get-tuple-element.108), channel_id=1, source_target_pairs={{0,1},{1,0},{2,3},{3,2},{4,5},{5,4},{6,7},{7,6},{8,9},{9,8},{10,11... | collective-permute-start | bytes 2359304 | tf_op jit(solution)/shard_map/ppermute | solution.py:603
  146.8 7.7 %collective-permute-start.23 = (bf16[4,64,1152]{2,1,0:T(8,128)(2,1)S(1)}, bf16[4,64,1152]{2,1,0:T(8,128)(2,1)S(1)}, u32[]{:S(2)}, u32[]{:S(2)}) collective-permute-start(bf16[4,64,1152]{2,1,0:T(8,128)(2,1)S(1)} %get-tuple-element.142), channel_id=1, source_target_pairs={{0,2},{1,5},{2,0},{3,7},{4,6},{5,1},{6,4},{7,3},{8,10},{9,13},{10,... | collective-permute-start | bytes 1769480 | tf_op jit(solution)/shard_map/ppermute | solution.py:603
  159.5 3.7 %shard_map.443 = (f32[1024,512]{1,0:T(8,128)S(1)}, bf16[1024,512]{1,0:T(8,128)(2,1)S(1)}, f32[2,512]{1,0:T(2,128)S(1)}) custom-call(s32[4]{0:T(128)S(1)} %copy-done.14, bf16[1024,512]{1,0:T(8,128)(2,1)S(1)} %copy-done.6, bf16[1024,512]{1,0:T(8,128)(2,1)S(1)} %copy-done.8, f32[4,512]{1,0:T(4,128)S(1)} %copy-done.11, bf16[3,512,512]{2,1,0:T(8,128)(2,1)S(1)} %copy-done.4, ...), custom_call_target="tpu_custom_call" | custom-call | flops 2684354560 | bytes 14680064 | tf_op jit(solution)/shard_map/pallas_call | solution.py:49
  163.1 2.5 %collective-permute-done.23 = bf16[4,64,1152]{2,1,0:T(8,128)(2,1)S(1)} collective-permute-done((bf16[4,64,1152]{2,1,0:T(8,128)(2,1)S(1)}, bf16[4,64,1152]{2,1,0:T(8,128)(2,1)S(1)}, u32[]{:S(2)}, u32[]{:S(2)}) %collective-permute-start.23) | collective-permute-done | bytes 589856 | tf_op jit(solution)/shard_map/ppermute | solution.py:603
  165.8 5.8 %collective-permute-start.33 = (bf16[64,1152]{1,0:T(8,128)(2,1)S(1)}, bf16[64,1152]{1,0:T(8,128)(2,1)S(1)}, u32[]{:S(2)}, u32[]{:S(2)}) collective-permute-start(bf16[64,1152]{1,0:T(8,128)(2,1)S(1)} %get-tuple-element.146), channel_id=1, source_target_pairs={{0,24},{1,25},{2,26},{3,27},{4,28},{5,29},{6,30},{7,31},{8,16},{9,... | collective-permute-start | bytes 442376 | tf_op jit(solution)/shard_map/ppermute | solution.py:603
  172.3 2.5 %collective-permute-start.27 = (bf16[4,3,64,128]{3,2,1,0:T(8,128)(2,1)S(1)}, bf16[4,3,64,128]{3,2,1,0:T(8,128)(2,1)S(1)}, u32[]{:S(2)}, u32[]{:S(2)}) collective-permute-start(bf16[4,3,64,128]{3,2,1,0:T(8,128)(2,1)S(1)} %get-tuple-element.149), channel_id=1, source_target_pairs={{0,2},{1,5},{2,0},{3,7},{4,6},{5,1},{6,4},{7,3},{8,10},{9,13},{10,... | collective-permute-start | bytes 589832 | tf_op jit(solution)/shard_map/ppermute | solution.py:603
  176.5 6.2 %collective-permute-done.32 = bf16[64,1152]{1,0:T(8,128)(2,1)S(1)} collective-permute-done((bf16[64,1152]{1,0:T(8,128)(2,1)S(1)}, bf16[64,1152]{1,0:T(8,128)(2,1)S(1)}, u32[]{:S(2)}, u32[]{:S(2)}) %collective-permute-start.32) | collective-permute-done | bytes 147488 | tf_op jit(solution)/shard_map/ppermute | solution.py:603
  183.4 2.8 %collective-permute-start.30 = (bf16[3,64,128]{2,1,0:T(8,128)(2,1)S(1)}, bf16[3,64,128]{2,1,0:T(8,128)(2,1)S(1)}, u32[]{:S(2)}, u32[]{:S(2)}) collective-permute-start(bf16[3,64,128]{2,1,0:T(8,128)(2,1)S(1)} %get-tuple-element.151), channel_id=1, source_target_pairs={{0,24},{1,25},{2,26},{3,27},{4,28},{5,29},{6,30},{7,31},{8,16},{9,... | collective-permute-start | bytes 147464 | tf_op jit(solution)/shard_map/ppermute | solution.py:603
  189.7 2.1 collective-permute-done.29
  197.1 3.4 %collective-permute-start.37 = (f32[8,512]{1,0:T(8,128)S(1)}, f32[8,512]{1,0:T(8,128)S(1)}, u32[]{:S(2)}, u32[]{:S(2)}) collective-permute-start(f32[8,512]{1,0:T(8,128)S(1)} %fusion.30), channel_id=1, source_target_pairs={{0,6},{1,7},{2,4},{3,5},{4,2},{5,3},{6,0},{7,1},{8,14},{9,15},{10,... | collective-permute-start | bytes 49160 | tf_op jit(solution)/shard_map/ppermute | solution.py:603
  223.5 2.9 %convert_add_fusion = f32[1024,512]{1,0:T(8,128)} fusion(f32[1024,512]{1,0:T(8,128)S(1)} %get-tuple-element.105, bf16[1024,512]{1,0:T(8,128)(2,1)} %collective-permute-done.26), kind=kLoop, calls=%fused_computation.2 | loop fusion | flops 1048576 | bytes 5242880 | tf_op jit(solution)/shard_map/add | solution.py:818
  (185 shorter events, 59.3 us)
Async XLA Ops:
  0.7 13.2 %collective-permute-start.3 = (bf16[1024,512]{1,0:T(8,128)(2,1)}, bf16[1024,512]{1,0:T(8,128)(2,1)S(1)}, u32[]{:S(2)}, u32[]{:S(2)}) collective-permute-start(bf16[1024,512]{1,0:T(8,128)(2,1)} %own_ref.1), channel_id=1, source_target_pairs={{0,1},{1,2},{2,3},{4,5},{5,6},{6,7},{8,9},{9,10},{10,11},{12,13},{... | collective-permute-start | bytes 3145736 | tf_op jit(solution)/shard_map/ppermute | solution.py:741
  4.2 8.6 %collective-permute-start.2 = (bf16[3,64,128]{2,1,0:T(8,128)(2,1)S(1)}, bf16[3,64,128]{2,1,0:T(8,128)(2,1)S(1)}, u32[]{:S(2)}, u32[]{:S(2)}) collective-permute-start(bf16[3,64,128]{2,1,0:T(8,128)(2,1)S(1)} %convert_element_type.252), channel_id=1, source_target_pairs={{0,24},{1,25},{2,26},{3,27},{4,28},{5,29},{6,30},{7,31},{8,16},{9,... | collective-permute-start | bytes 147464 | tf_op jit(solution)/shard_map/ppermute | solution.py:603
  14.0 12.1 %collective-permute-start.7 = (bf16[4,3,64,128]{3,2,1,0:T(8,128)(2,1)S(1)}, bf16[4,3,64,128]{3,2,1,0:T(8,128)(2,1)S(1)}, u32[]{:S(2)}, u32[]{:S(2)}) collective-permute-start(bf16[4,3,64,128]{3,2,1,0:T(8,128)(2,1)S(1)} %pad_maximum_fusion.1.refs_4_), channel_id=1, source_target_pairs={{0,2},{1,5},{2,0},{3,7},{4,6},{5,1},{6,4},{7,3},{8,10},{9,13},{10,... | collective-permute-start | bytes 589832 | tf_op jit(solution)/shard_map/ppermute | solution.py:603
  20.1 6.0 %collective-permute-start.8 = (bf16[4,3,64,128]{3,2,1,0:T(8,128)(2,1)S(1)}, bf16[4,3,64,128]{3,2,1,0:T(8,128)(2,1)S(1)}, u32[]{:S(2)}, u32[]{:S(2)}) collective-permute-start(bf16[4,3,64,128]{3,2,1,0:T(8,128)(2,1)S(1)} %pad_maximum_fusion.1.refs_4_), channel_id=1, source_target_pairs={{0,4},{1,3},{2,6},{3,1},{4,0},{5,7},{6,2},{7,5},{8,12},{9,11},{10,... | collective-permute-start | bytes 589832 | tf_op jit(solution)/shard_map/ppermute | solution.py:603
  21.6 8.5 %collective-permute-start.6 = (bf16[64,1152]{1,0:T(8,128)(2,1)S(1)}, bf16[64,1152]{1,0:T(8,128)(2,1)S(1)}, u32[]{:S(2)}, u32[]{:S(2)}) collective-permute-start(bf16[64,1152]{1,0:T(8,128)(2,1)S(1)} %pad_maximum_fusion.2), channel_id=1, source_target_pairs={{0,24},{1,25},{2,26},{3,27},{4,28},{5,29},{6,30},{7,31},{8,16},{9,... | collective-permute-start | bytes 442376 | tf_op jit(solution)/shard_map/ppermute | solution.py:603
  25.3 10.1 %collective-permute-start.5 = (bf16[64,1152]{1,0:T(8,128)(2,1)S(1)}, bf16[64,1152]{1,0:T(8,128)(2,1)S(1)}, u32[]{:S(2)}, u32[]{:S(2)}) collective-permute-start(bf16[64,1152]{1,0:T(8,128)(2,1)S(1)} %pad_maximum_fusion.2), channel_id=1, source_target_pairs={{0,16},{1,17},{2,18},{3,19},{4,20},{5,21},{6,22},{7,23},{8,24},{9,... | collective-permute-start | bytes 442376 | tf_op jit(solution)/shard_map/ppermute | solution.py:603
  25.3 10.1 %collective-permute-start.4 = (bf16[64,1152]{1,0:T(8,128)(2,1)S(1)}, bf16[64,1152]{1,0:T(8,128)(2,1)S(1)}, u32[]{:S(2)}, u32[]{:S(2)}) collective-permute-start(bf16[64,1152]{1,0:T(8,128)(2,1)S(1)} %pad_maximum_fusion.2), channel_id=1, source_target_pairs={{0,8},{1,9},{2,10},{3,11},{4,12},{5,13},{6,14},{7,15},{8,0},{9,1},... | collective-permute-start | bytes 442376 | tf_op jit(solution)/shard_map/ppermute | solution.py:603
  26.1 10.2 %collective-permute-start.9 = (bf16[4,3,64,128]{3,2,1,0:T(8,128)(2,1)S(1)}, bf16[4,3,64,128]{3,2,1,0:T(8,128)(2,1)S(1)}, u32[]{:S(2)}, u32[]{:S(2)}) collective-permute-start(bf16[4,3,64,128]{3,2,1,0:T(8,128)(2,1)S(1)} %collective-permute-done.7.refs_5_), channel_id=1, source_target_pairs={{0,4},{1,3},{2,6},{3,1},{4,0},{5,7},{6,2},{7,5},{8,12},{9,11},{10,... | collective-permute-start | bytes 589832 | tf_op jit(solution)/shard_map/ppermute | solution.py:603
  37.0 16.3 %collective-permute-start.10 = (bf16[4,64,1152]{2,1,0:T(8,128)(2,1)}, bf16[4,64,1152]{2,1,0:T(8,128)(2,1)}, u32[]{:S(2)}, u32[]{:S(2)}) collective-permute-start(bf16[4,64,1152]{2,1,0:T(8,128)(2,1)} %pad_maximum_fusion.refs_7_), channel_id=1, source_target_pairs={{0,2},{1,5},{2,0},{3,7},{4,6},{5,1},{6,4},{7,3},{8,10},{9,13},{10,... | collective-permute-start | bytes 1769480 | tf_op jit(solution)/shard_map/ppermute | solution.py:603
  38.8 14.6 %collective-permute-start.11 = (bf16[4,64,1152]{2,1,0:T(8,128)(2,1)}, bf16[4,64,1152]{2,1,0:T(8,128)(2,1)}, u32[]{:S(2)}, u32[]{:S(2)}) collective-permute-start(bf16[4,64,1152]{2,1,0:T(8,128)(2,1)} %pad_maximum_fusion.refs_7_), channel_id=1, source_target_pairs={{0,4},{1,3},{2,6},{3,1},{4,0},{5,7},{6,2},{7,5},{8,12},{9,11},{10,... | collective-permute-start | bytes 1769480 | tf_op jit(solution)/shard_map/ppermute | solution.py:603
  40.9 29.7 %collective-permute-start.17 = (bf16[4,64,1152]{2,1,0:T(8,128)(2,1)}, bf16[4,64,1152]{2,1,0:T(8,128)(2,1)}, u32[]{:S(2)}, u32[]{:S(2)}) collective-permute-start(bf16[4,64,1152]{2,1,0:T(8,128)(2,1)} %pad_maximum_fusion.refs_7_), channel_id=1, source_target_pairs={{0,1},{1,0},{2,3},{3,2},{4,5},{5,4},{6,7},{7,6},{8,9},{9,8},{10,11... | collective-permute-start | bytes 1769480 | tf_op jit(solution)/shard_map/ppermute | solution.py:603
  53.3 15.6 %collective-permute-start.16 = (bf16[4,64,1152]{2,1,0:T(8,128)(2,1)}, bf16[4,64,1152]{2,1,0:T(8,128)(2,1)S(1)}, u32[]{:S(2)}, u32[]{:S(2)}) collective-permute-start(bf16[4,64,1152]{2,1,0:T(8,128)(2,1)} %collective-permute-done.10.refs_8_), channel_id=1, source_target_pairs={{0,4},{1,3},{2,6},{3,1},{4,0},{5,7},{6,2},{7,5},{8,12},{9,11},{10,... | collective-permute-start | bytes 1769480 | tf_op jit(solution)/shard_map/ppermute | solution.py:603
  53.6 17.0 %collective-permute-start.18 = (bf16[4,64,1152]{2,1,0:T(8,128)(2,1)}, bf16[4,64,1152]{2,1,0:T(8,128)(2,1)S(1)}, u32[]{:S(2)}, u32[]{:S(2)}) collective-permute-start(bf16[4,64,1152]{2,1,0:T(8,128)(2,1)} %collective-permute-done.10.refs_8_), channel_id=1, source_target_pairs={{0,1},{1,0},{2,3},{3,2},{4,5},{5,4},{6,7},{7,6},{8,9},{9,8},{10,11... | collective-permute-start | bytes 1769480 | tf_op jit(solution)/shard_map/ppermute | solution.py:603
  54.6 15.9 %collective-permute-start.19 = (bf16[4,64,1152]{2,1,0:T(8,128)(2,1)}, bf16[4,64,1152]{2,1,0:T(8,128)(2,1)S(1)}, u32[]{:S(2)}, u32[]{:S(2)}) collective-permute-start(bf16[4,64,1152]{2,1,0:T(8,128)(2,1)} %collective-permute-done.11.refs_9_), channel_id=1, source_target_pairs={{0,1},{1,0},{2,3},{3,2},{4,5},{5,4},{6,7},{7,6},{8,9},{9,8},{10,11... | collective-permute-start | bytes 1769480 | tf_op jit(solution)/shard_map/ppermute | solution.py:603
  110.1 31.7 %collective-permute-start.22 = (bf16[8,64,1152]{2,1,0:T(8,128)(2,1)S(1)}, bf16[8,64,1152]{2,1,0:T(8,128)(2,1)S(1)}, u32[]{:S(2)}, u32[]{:S(2)}) collective-permute-start(bf16[8,64,1152]{2,1,0:T(8,128)(2,1)S(1)} %get-tuple-element.140), channel_id=1, source_target_pairs={{0,4},{1,3},{2,6},{3,1},{4,0},{5,7},{6,2},{7,5},{8,12},{9,11},{10,... | collective-permute-start | bytes 3538952 | tf_op jit(solution)/shard_map/ppermute | solution.py:603
  141.9 12.6 %collective-permute-start.24 = (bf16[16,3,64,128]{3,2,1,0:T(8,128)(2,1)}, bf16[16,3,64,128]{3,2,1,0:T(8,128)(2,1)S(1)}, u32[]{:S(2)}, u32[]{:S(2)}) collective-permute-start(bf16[16,3,64,128]{3,2,1,0:T(8,128)(2,1)} %get-tuple-element.108), channel_id=1, source_target_pairs={{0,1},{1,0},{2,3},{3,2},{4,5},{5,4},{6,7},{7,6},{8,9},{9,8},{10,11... | collective-permute-start | bytes 2359304 | tf_op jit(solution)/shard_map/ppermute | solution.py:603
  146.8 18.9 %collective-permute-start.23 = (bf16[4,64,1152]{2,1,0:T(8,128)(2,1)S(1)}, bf16[4,64,1152]{2,1,0:T(8,128)(2,1)S(1)}, u32[]{:S(2)}, u32[]{:S(2)}) collective-permute-start(bf16[4,64,1152]{2,1,0:T(8,128)(2,1)S(1)} %get-tuple-element.142), channel_id=1, source_target_pairs={{0,2},{1,5},{2,0},{3,7},{4,6},{5,1},{6,4},{7,3},{8,10},{9,13},{10,... | collective-permute-start | bytes 1769480 | tf_op jit(solution)/shard_map/ppermute | solution.py:603
  155.8 9.8 %collective-permute-start.25 = (bf16[8,3,64,128]{3,2,1,0:T(8,128)(2,1)S(1)}, bf16[8,3,64,128]{3,2,1,0:T(8,128)(2,1)S(1)}, u32[]{:S(2)}, u32[]{:S(2)}) collective-permute-start(bf16[8,3,64,128]{3,2,1,0:T(8,128)(2,1)S(1)} %get-tuple-element.144), channel_id=1, source_target_pairs={{0,4},{1,3},{2,6},{3,1},{4,0},{5,7},{6,2},{7,5},{8,12},{9,11},{10,... | collective-permute-start | bytes 1179656 | tf_op jit(solution)/shard_map/ppermute | solution.py:603
  165.8 10.7 %collective-permute-start.33 = (bf16[64,1152]{1,0:T(8,128)(2,1)S(1)}, bf16[64,1152]{1,0:T(8,128)(2,1)S(1)}, u32[]{:S(2)}, u32[]{:S(2)}) collective-permute-start(bf16[64,1152]{1,0:T(8,128)(2,1)S(1)} %get-tuple-element.146), channel_id=1, source_target_pairs={{0,24},{1,25},{2,26},{3,27},{4,28},{5,29},{6,30},{7,31},{8,16},{9,... | collective-permute-start | bytes 442376 | tf_op jit(solution)/shard_map/ppermute | solution.py:603
  171.6 11.0 %collective-permute-start.32 = (bf16[64,1152]{1,0:T(8,128)(2,1)S(1)}, bf16[64,1152]{1,0:T(8,128)(2,1)S(1)}, u32[]{:S(2)}, u32[]{:S(2)}) collective-permute-start(bf16[64,1152]{1,0:T(8,128)(2,1)S(1)} %get-tuple-element.147), channel_id=1, source_target_pairs={{0,16},{1,17},{2,18},{3,19},{4,20},{5,21},{6,22},{7,23},{8,24},{9,... | collective-permute-start | bytes 442376 | tf_op jit(solution)/shard_map/ppermute | solution.py:603
  171.6 11.0 %collective-permute-start.31 = (bf16[64,1152]{1,0:T(8,128)(2,1)S(1)}, bf16[64,1152]{1,0:T(8,128)(2,1)S(1)}, u32[]{:S(2)}, u32[]{:S(2)}) collective-permute-start(bf16[64,1152]{1,0:T(8,128)(2,1)S(1)} %get-tuple-element.145), channel_id=1, source_target_pairs={{0,8},{1,9},{2,10},{3,11},{4,12},{5,13},{6,14},{7,15},{8,0},{9,1},... | collective-permute-start | bytes 442376 | tf_op jit(solution)/shard_map/ppermute | solution.py:603
  172.3 11.0 %collective-permute-start.27 = (bf16[4,3,64,128]{3,2,1,0:T(8,128)(2,1)S(1)}, bf16[4,3,64,128]{3,2,1,0:T(8,128)(2,1)S(1)}, u32[]{:S(2)}, u32[]{:S(2)}) collective-permute-start(bf16[4,3,64,128]{3,2,1,0:T(8,128)(2,1)S(1)} %get-tuple-element.149), channel_id=1, source_target_pairs={{0,2},{1,5},{2,0},{3,7},{4,6},{5,1},{6,4},{7,3},{8,10},{9,13},{10,... | collective-permute-start | bytes 589832 | tf_op jit(solution)/shard_map/ppermute | solution.py:603
  183.4 6.2 %collective-permute-start.30 = (bf16[3,64,128]{2,1,0:T(8,128)(2,1)S(1)}, bf16[3,64,128]{2,1,0:T(8,128)(2,1)S(1)}, u32[]{:S(2)}, u32[]{:S(2)}) collective-permute-start(bf16[3,64,128]{2,1,0:T(8,128)(2,1)S(1)} %get-tuple-element.151), channel_id=1, source_target_pairs={{0,24},{1,25},{2,26},{3,27},{4,28},{5,29},{6,30},{7,31},{8,16},{9,... | collective-permute-start | bytes 147464 | tf_op jit(solution)/shard_map/ppermute | solution.py:603
  208.6 14.9 %collective-permute-start.26 = (bf16[1024,512]{1,0:T(8,128)(2,1)S(1)}, bf16[1024,512]{1,0:T(8,128)(2,1)}, u32[]{:S(2)}, u32[]{:S(2)}) collective-permute-start(bf16[1024,512]{1,0:T(8,128)(2,1)S(1)} %get-tuple-element.110), channel_id=1, source_target_pairs={{1,0},{2,1},{3,2},{5,4},{6,5},{7,6},{9,8},{10,9},{11,10},{13,12},{... | collective-permute-start | bytes 3145736 | tf_op jit(solution)/shard_map/ppermute | solution.py:741
  (57 other events, 640.3 us)
